TPU v7x, 32 devices: a whole 2x2x4 slice. The times are simulated.
32 devices in a mesh: member: 2 (over y), lon: 4 (over z), lat: 2 (over x), dp: 2 (over core).
Axes of the slice: x: 2, y: 2, z: 4, core: 2. Of those that a mesh axis runs over, the one named last changes fastest.
Arguments:
- fields: bfloat16 [4, 64, 32, 512], P(('member', 'dp'), 'lat', 'lon'), parts along dimension 0, may hold values from -6 to 6
- cotangent: bfloat16 [4, 64, 32, 512], P(('member', 'dp'), 'lat', 'lon'), parts along dimension 0, may hold values from -6 to 6
- conv_weight: float32 [7, 7, 512], replicated, may hold values from -0.875 to 0.875
- norm_gain: float32 [512], replicated, may hold values from 0.1 to 1.9
- w_qkv: bfloat16 [512, 768], replicated, may hold values from -1 to 1
- w_out: bfloat16 [256, 512], replicated, may hold values from -0.375 to 0.375
Outputs:
- result: bfloat16 [4, 64, 32, 512], P(('member', 'dp'), 'lat', 'lon'), parts along dimension 0
- grad_fields: bfloat16 [4, 64, 32, 512], P(('member', 'dp'), 'lat', 'lon'), parts along dimension 0
- grad_qkv: float32 [1024, 768], P('member'), parts along dimension 0
- grad_out: float32 [512, 512], P('member'), parts along dimension 0
- grad_conv: float32 [14, 7, 512], P('member'), parts along dimension 0
- grad_gain: float32 [1024], P('member'), parts along dimension 0
There are 2 independent parts, one for each index of `member`. A program takes and returns all parts, laid end to end along the dimension named above; an argument that names none is the same for every part. Nothing has to cross between parts.
All inputs are finite; a program needn't handle non-finite values.
Results may differ from a plain program's by a relative error of at most 0.012.
The roundings to bfloat16 on the way count: a program that leaves them out, or rounds other values in their place, can miss the bound.
Values may be sent and summed in bfloat16 or wider, within the bound.
A program may use at most 64 MiB of HBM per device.

v0:
```python
import jax
import jax.numpy as jnp
from jax import lax
from jax.sharding import PartitionSpec as P

HEADS = 4
HEAD_DIM = 64


EPSILON = 1e-06


def with_halo(x, sides, width, wrap):
    for axis, dim in sides:
        size, length = (lax.axis_size(axis), x.shape[dim])
        up = [(i, (i + 1) % size) for i in range(size if wrap else size - 1)]
        down = [(j, i) for i, j in up]
        last = lax.slice_in_dim(x, length - width, length, axis=dim)
        first = lax.slice_in_dim(x, 0, width, axis=dim)
        before = lax.ppermute(last, axis, up)
        after = lax.ppermute(first, axis, down)
        x = jnp.concatenate([before, x, after], axis=dim)
    return x


def spread(padded, kernel, lat_rows, lon_cols):
    summed = jnp.zeros(padded.shape[:1] + (lat_rows, lon_cols, padded.shape[3]), jnp.float32)
    for row_shift in range(7):
        band = padded[:, row_shift : row_shift + lat_rows].astype(jnp.float32)
        partial_row = kernel[row_shift, 0] * band[:, :, 0:lon_cols]
        for col_shift in range(1, 7):
            partial_row = (
                partial_row
                + kernel[row_shift, col_shift] * band[:, :, col_shift : col_shift + lon_cols]
            )
        summed = summed + partial_row
    return summed


def correlate(padded, upstream, lat_rows, lon_cols):
    pieces = []
    for row_shift in range(7):
        for col_shift in range(7):
            window = padded[
                :, row_shift : row_shift + lat_rows, col_shift : col_shift + lon_cols
            ].astype(jnp.float32)
            pieces.append(jnp.sum(window * upstream, axis=(0, 1, 2)))
    return jnp.stack(pieces).reshape(7, 7, -1)


def split_heads(values):
    return values.reshape(values.shape[:-1] + (HEADS, HEAD_DIM))


def attend_forward(rowwise, att_width):
    queries = split_heads(rowwise[..., :att_width])
    keys_part = split_heads(rowwise[..., att_width : 2 * att_width])
    values_part = split_heads(rowwise[..., 2 * att_width :])
    scores = jnp.einsum(
        "brqhd,brkhd->brhqk", queries, keys_part, preferred_element_type=jnp.float32
    ) * HEAD_DIM ** (-0.5)
    row_peak = jnp.max(scores, -1, keepdims=True)
    raised = jnp.exp(scores - row_peak)
    probs = raised / jnp.sum(raised, -1, keepdims=True)
    weights = probs.astype(jnp.bfloat16)
    mixed = jnp.einsum(
        "brhqk,brkhd->brqhd", weights, values_part, preferred_element_type=jnp.float32
    )
    return (mixed.reshape(rowwise.shape[:3] + (att_width,)).astype(jnp.bfloat16), probs)


def attend_backward(rowwise, probs, grad_rowwise, att_width):
    queries = split_heads(rowwise[..., :att_width])
    keys_part = split_heads(rowwise[..., att_width : 2 * att_width])
    values_part = split_heads(rowwise[..., 2 * att_width :])
    grad_heads = split_heads(grad_rowwise)
    weights = probs.astype(jnp.bfloat16)
    grad_probs = jnp.einsum(
        "brqhd,brkhd->brhqk", grad_heads, values_part, preferred_element_type=jnp.float32
    )
    inner = jnp.sum(probs * grad_probs, -1, keepdims=True)
    grad_scores = (probs * (grad_probs - inner) * HEAD_DIM ** (-0.5)).astype(jnp.bfloat16)
    grad_query = jnp.einsum(
        "brhqk,brkhd->brqhd", grad_scores, keys_part, preferred_element_type=jnp.float32
    )
    grad_key = jnp.einsum(
        "brhqk,brqhd->brkhd", grad_scores, queries, preferred_element_type=jnp.float32
    )
    grad_value = jnp.einsum(
        "brhqk,brqhd->brkhd", weights, grad_heads, preferred_element_type=jnp.float32
    )
    shaped = rowwise.shape[:3] + (att_width,)
    return jnp.concatenate(
        [
            grad_query.reshape(shaped).astype(jnp.bfloat16),
            grad_key.reshape(shaped).astype(jnp.bfloat16),
            grad_value.reshape(shaped).astype(jnp.bfloat16),
        ],
        axis=-1,
    )


def contract_rows(left, right):
    return lax.dot_general(
        left, right, (((0,), (0,)), ((), ())), preferred_element_type=jnp.float32
    )


def contract_cols(left, right):
    return lax.dot_general(
        left, right, (((1,), (1,)), ((), ())), preferred_element_type=jnp.float32
    )


def on_device(fields, cotangent, conv_weight, norm_gain, w_qkv, w_out):
    batch_count, lat_rows, lon_cols, channels = fields.shape
    att_width = w_out.shape[0]
    wide = with_halo(fields, (("lon", 2),), 3, True)
    padded = with_halo(wide, (("lat", 1),), 3, False)
    update = fields.astype(jnp.float32) + spread(padded, conv_weight, lat_rows, lon_cols)
    inverse = lax.rsqrt(jnp.mean(update * update, -1, keepdims=True) + EPSILON)
    normed = (update * inverse * norm_gain).astype(jnp.bfloat16)
    normed_flat = normed.reshape(-1, channels)
    projected = jnp.dot(normed_flat, w_qkv, preferred_element_type=jnp.float32).astype(jnp.bfloat16)
    rowwise = lax.all_to_all(
        projected.reshape(batch_count, lat_rows, lon_cols, 3 * att_width),
        "lon",
        split_axis=1,
        concat_axis=2,
        tiled=True,
    )
    mixed_rows, probs = attend_forward(rowwise, att_width)
    mixed = lax.all_to_all(mixed_rows, "lon", split_axis=2, concat_axis=1, tiled=True)
    mixed_flat = mixed.reshape(-1, att_width)
    result = (
        update
        + jnp.dot(mixed_flat, w_out, preferred_element_type=jnp.float32).reshape(update.shape)
    ).astype(jnp.bfloat16)
    upstream_flat = cotangent.reshape(-1, channels)
    grad_mixed = contract_cols(upstream_flat, w_out).astype(jnp.bfloat16)
    grad_out = contract_rows(mixed_flat, upstream_flat)
    grad_rowwise = lax.all_to_all(
        grad_mixed.reshape(batch_count, lat_rows, lon_cols, att_width),
        "lon",
        split_axis=1,
        concat_axis=2,
        tiled=True,
    )
    grad_projected_rows = attend_backward(rowwise, probs, grad_rowwise, att_width)
    grad_projected = lax.all_to_all(
        grad_projected_rows, "lon", split_axis=2, concat_axis=1, tiled=True
    )
    grad_flat = grad_projected.reshape(-1, 3 * att_width)
    grad_weight = contract_rows(normed_flat, grad_flat)
    grad_normed = contract_cols(grad_flat, w_qkv).reshape(update.shape)
    grad_gain = jnp.sum(grad_normed * (update * inverse), axis=(0, 1, 2))
    gained = norm_gain * grad_normed
    grad_update = (
        cotangent.astype(jnp.float32)
        + inverse * gained
        - update * inverse**3 * jnp.mean(gained * update, -1, keepdims=True)
    )
    grad_wide = with_halo(grad_update.astype(jnp.bfloat16), (("lon", 2),), 3, True).astype(
        grad_update.dtype
    )
    grad_padded = with_halo(grad_wide.astype(jnp.bfloat16), (("lat", 1),), 3, False).astype(
        grad_wide.dtype
    )
    grad_fields = (
        grad_update + spread(grad_padded, conv_weight[::-1, ::-1], lat_rows, lon_cols)
    ).astype(jnp.bfloat16)
    grad_conv = correlate(padded, grad_update, lat_rows, lon_cols)
    totals = lax.psum((grad_weight, grad_out, grad_conv, grad_gain), ("lon", "lat", "dp"))
    return (result, grad_fields, totals[0], totals[1], totals[2], totals[3])


def solution(mesh):
    placed = (
        P(("member", "dp"), "lat", "lon", None),
        P(("member", "dp"), "lat", "lon", None),
        P(),
        P(),
        P(),
        P(),
    )
    return jax.shard_map(
        on_device,
        mesh=mesh,
        in_specs=placed,
        out_specs=(
            P(("member", "dp"), "lat", "lon", None),
            P(("member", "dp"), "lat", "lon", None),
            P("member", None),
            P("member", None),
            P("member", None, None),
            P("member"),
        ),
        check_vma=False,
    )
```

profile of v0, /device:TPU:0, one launch (start us, length us, event | category | flops | bytes accessed | tf_op | source)
XLA Modules:
  0.0 233.1 jit_solution(6971295654083758024)
XLA Ops:
  7.2 1.2 fusion.160
  8.4 3.1 %collective-permute-start = (bf16[1,32,3,512]{3,2,1,0:T(4,128)(2,1)S(1)}, bf16[1,32,3,512]{3,2,1,0:T(4,128)(2,1)S(1)}, u32[]{:S(2)}, u32[]{:S(2)}) collective-permute-start(bf16[1,32,3,512]{3,2,1,0:T(4,128)(2,1)S(1)} %get-tuple-element.93), channel_id=1, source_target_pairs={{0,4},{4,8},{8,12},{12,0},{1,5},{5,9},{9,13},{13,1},{2,6},{6,10},{... | collective-permute-start | bytes 294920 | tf_op jit(solution)/shard_map/ppermute | solution.py:20
  11.6 2.1 collective-permute-start.1
  13.6 1.9 fusion.15
  15.6 3.9 %all-to-all-start.2 = ((bf16[1,32,8,256]{3,2,0,1:T(8,128)(2,1)}), bf16[1,32,8,256]{3,2,0,1:T(8,128)(2,1)}, u32[]{:S(2)}, u32[]{:S(2)}) async-start(bf16[1,32,8,256]{3,2,0,1:T(8,128)(2,1)} %fusion.15), calls=%async_computation.2 | async-start | bytes 262144 | tf_op jit(solution)/shard_map/all_to_all | solution.py:142
  19.6 0.6 fusion.161
  20.2 0.7 fusion.162
  20.9 1.2 fusion.156
  22.1 3.5 %collective-permute-start.2 = (bf16[1,3,14,512]{3,2,1,0:T(8,128)(2,1)S(1)}, bf16[1,3,14,512]{3,2,1,0:T(8,128)(2,1)S(1)}, u32[]{:S(2)}, u32[]{:S(2)}) collective-permute-start(bf16[1,3,14,512]{3,2,1,0:T(8,128)(2,1)S(1)} %get-tuple-element.84), channel_id=1, source_target_pairs={{0,2},{1,3},{4,6},{5,7},{8,10},{9,11},{12,14},{13,15},{16,18},{17,... | collective-permute-start | bytes 129032 | tf_op jit(solution)/shard_map/ppermute | solution.py:20
  25.7 1.3 collective-permute-start.3
  27.0 0.6 fusion.163
  27.6 4.0 %collective-permute-done.3 = bf16[1,3,14,512]{3,2,1,0:T(8,128)(2,1)S(1)} collective-permute-done((bf16[1,3,14,512]{3,2,1,0:T(8,128)(2,1)S(1)}, bf16[1,3,14,512]{3,2,1,0:T(8,128)(2,1)S(1)}, u32[]{:S(2)}, u32[]{:S(2)}) %collective-permute-start.3) | collective-permute-done | bytes 43040 | tf_op jit(solution)/shard_map/ppermute | solution.py:21
  31.7 0.3 maximum_maximum_fusion
  32.0 2.0 slice_convert_fusion.2
  34.0 10.5 %multiply_reduce_fusion.51 = (f32[32,8]{1,0:T(8,128)S(1)}, f32[1,32,8,512]{3,2,1,0:T(8,128)S(1)}) fusion(f32[1,32,14,512]{3,2,1,0:T(8,128)S(1)} %get-tuple-element.77, f32[512]{0:T(512)} %bitcast.283, f32[512]{0:T(512)} %bitcast.285, f32[512]{0:T(512)S(1)} %bitcast.191, f32[512]{0:T(512)S(1)} %bitcast.193, f32[512]{0:T(512)S(1)} %bitcast.195, ...), kind=kLoop, calls=%fused_computation.293 | loop fusion | flops 13238016 | bytes 26577920 | tf_op jit(solution)/shard_map/reduce_sum | solution.py:121
  44.6 1.2 fusion.10
  45.7 5.0 %all-to-all-start = ((bf16[1,32,8,768]{3,2,0,1:T(8,128)(2,1)}), bf16[1,32,8,768]{3,2,0,1:T(8,128)(2,1)S(1)}, u32[]{:S(2)}, u32[]{:S(2)}) async-start(bf16[1,32,8,768]{3,2,0,1:T(8,128)(2,1)} %fusion.10), calls=%async_computation | async-start | bytes 786432 | tf_op jit(solution)/shard_map/all_to_all | solution.py:125
  50.8 0.7 constant_dynamic-update-slice_fusion.1
  51.5 1.6 copy.83
  53.1 1.1 reshape.613
  54.2 6.2 %all-to-all-done = bf16[1,32,8,768]{3,2,0,1:T(8,128)(2,1)S(1)} async-done(((bf16[1,32,8,768]{3,2,0,1:T(8,128)(2,1)}), bf16[1,32,8,768]{3,2,0,1:T(8,128)(2,1)S(1)}, u32[]{:S(2)}, u32[]{:S(2)}) %all-to-all-start) | async-done | bytes 393248 | tf_op jit(solution)/shard_map/all_to_all | solution.py:125
  60.4 0.9 reshape.608
  61.3 0.9 reshape.609
  62.3 2.1 fusion.164
  64.5 1.1 fusion.129
  65.5 2.0 fusion.14
  67.5 1.0 fusion.11
  68.6 2.6 %fusion.12 = bf16[1,8,32,4,64]{4,2,3,1,0:T(8,128)(2,1)} fusion(f32[8,4,32,32]{2,3,1,0:T(8,128)} %fusion.129, bf16[8,32,4,64]{3,2,1,0:T(4,128)(2,1)S(1)} %copy-done.18, f32[8,4,32,32]{2,3,1,0:T(8,128)} %get-tuple-element.147, f32[8,4,32]{2,1,0:T(4,128)S(1)} %get-tuple-element.146), kind=kOutput, calls=%fused_computation.20 | convolution fusion | flops 4490271 | bytes 528384 | tf_op jit(solution)/shard_map/brhqk,brkhd->brqhd/dot_general | solution.py:83
  71.2 1.1 copy.88
  72.3 0.9 convert_element_type.322
  73.2 1.1 copy.99
  74.3 0.9 reshape.619
  75.1 3.9 %all-to-all-start.1 = ((bf16[1,8,32,256]{3,1,0,2:T(8,128)(2,1)}), bf16[1,8,32,256]{3,1,0,2:T(8,128)(2,1)}, u32[]{:S(2)}, u32[]{:S(2)}) async-start(bf16[1,8,32,256]{3,1,0,2:T(8,128)(2,1)} %reshape.619), calls=%async_computation.1 | async-start | bytes 262144 | tf_op jit(solution)/shard_map/all_to_all | solution.py:133
  79.1 2.6 %fusion.13 = bf16[1,8,32,4,64]{4,2,3,1,0:T(8,128)(2,1)} fusion(f32[8,4,32,32]{2,3,1,0:T(8,128)} %fusion.129, bf16[8,32,4,64]{3,2,1,0:T(4,128)(2,1)S(1)} %copy-done.17, f32[8,4,32,32]{2,3,1,0:T(8,128)} %get-tuple-element.147, f32[8,4,32]{2,1,0:T(4,128)S(1)} %get-tuple-element.146), kind=kOutput, calls=%fused_computation.21 | convolution fusion | flops 4490271 | bytes 528384 | tf_op jit(solution)/shard_map/brhqk,brqhd->brkhd/dot_general | solution.py:86
  81.7 1.1 copy.90
  82.8 0.9 convert_element_type.326
  83.6 1.1 copy.92
  84.7 0.9 convert_element_type.330
  85.6 1.1 pad_maximum_fusion.2
  86.7 1.0 copy.93
  87.6 5.0 %all-to-all-start.3 = ((bf16[1,8,32,768]{3,1,0,2:T(8,128)(2,1)}), bf16[1,8,32,768]{3,1,0,2:T(8,128)(2,1)S(1)}, u32[]{:S(2)}, u32[]{:S(2)}) async-start(bf16[1,8,32,768]{3,1,0,2:T(8,128)(2,1)} %copy.93), calls=%async_computation.3 | async-start | bytes 786432 | tf_op jit(solution)/shard_map/all_to_all | solution.py:150
  92.7 1.7 constant_dynamic-update-slice_fusion
  94.3 0.9 copy.134
  95.3 1.0 fusion.122
  96.3 0.9 fusion.9
  97.3 4.3 %all-to-all-done.3 = bf16[1,8,32,768]{3,1,0,2:T(8,128)(2,1)S(1)} async-done(((bf16[1,8,32,768]{3,1,0,2:T(8,128)(2,1)}), bf16[1,8,32,768]{3,1,0,2:T(8,128)(2,1)S(1)}, u32[]{:S(2)}, u32[]{:S(2)}) %all-to-all-start.3) | async-done | bytes 393248 | tf_op jit(solution)/shard_map/all_to_all | solution.py:150
  101.7 1.0 multiply_reduce_fusion.1
  102.7 2.2 multiply_reduce_fusion.2
  104.9 2.0 multiply_reduce_fusion.29
  107.0 0.6 collective-permute-start.4
  107.6 3.3 %collective-permute-start.5 = (bf16[1,32,3,512]{3,2,1,0:T(4,128)(2,1)S(1)}, bf16[1,32,3,512]{3,2,1,0:T(4,128)(2,1)S(1)}, u32[]{:S(2)}, u32[]{:S(2)}) collective-permute-start(bf16[1,32,3,512]{3,2,1,0:T(4,128)(2,1)S(1)} %get-tuple-element.92), channel_id=1, source_target_pairs={{4,0},{8,4},{12,8},{0,12},{5,1},{9,5},{13,9},{1,13},{6,2},{10,6},{... | collective-permute-start | bytes 294920 | tf_op jit(solution)/shard_map/ppermute | solution.py:21
  110.9 1.7 multiply_reduce_fusion.20
  112.6 1.4 collective-permute-done.4
  114.1 1.9 collective-permute-start.6
  116.3 1.3 collective-permute-start.7
  117.6 1.6 fusion.139
  119.9 0.7 reshape.617
  120.9 0.3 copy-done.93
  121.2 31.5 %psum.31 = f32[512]{0:T(512)} all-reduce(f32[512]{0:T(512)S(1)} %copy-done.93), channel_id=1, replica_groups=mesh['member'=2,'lon'=4,'lat'=2,'dp'=2] {'lon','lat','dp'}, use_global_device_ids=true, to_apply=%region_58.0 | all-reduce | flops 512 | bytes 4096 | tf_op jit(solution)/shard_map/psum | solution.py:173
  153.3 4.5 %fusion.24 = bf16[1,32,8,512]{3,2,1,0:T(8,128)(2,1)} fusion(f32[1,32,8,512]{3,2,1,0:T(8,128)S(1)} %get-tuple-element.70, f32[1,38,14,512]{3,2,1,0:T(8,128)S(1)} %maximum_convert_fusion, f32[512]{0:T(512)S(1)} %bitcast.284, f32[512]{0:T(512)S(1)} %bitcast.286, f32[512]{0:T(512)S(1)} %bitcast.192, f32[512]{0:T(512)S(1)} %bitcast.194, f32[512]{0:T(512)S(1)} %bitcast.196, ...), kind=kLoop, calls=%fused_computation.42 | loop fusion | flops 12976128 | bytes 26576896 | tf_op jit(solution)/shard_map/convert_element_type | solution.py:171
  157.8 64.3 %all-reduce.3.cloned.1.call-done = (f32[512,768]{1,0:T(8,128)}, f32[256,512]{1,0:T(8,128)}, f32[7,7,512]{2,1,0:T(8,128)}) async-done(((f32[512,768]{1,0:T(8,128)}, f32[256,512]{1,0:T(8,128)}, f32[7,7,512]{2,1,0:T(8,128)}), (f32[512,768]{1,0:T(8,128)}, f32[256,512]{1,0:T(8,128)}, f32[7,7,512]{2,1,0:T(8,128)})) %all-reduce.3.cloned.1.call-update) | async-done | bytes 2197520 | tf_op jit(solution)/shard_map/psum | solution.py:173
  222.1 2.7 %copy.139 = f32[512,768]{1,0:T(8,128)} copy(f32[512,768]{1,0:T(8,128)} %get-tuple-element.154) | data formatting | bytes 3145728
  224.8 0.8 copy.140
  225.6 0.6 copy.141
  (212 shorter events, 1.5 us)
Async XLA Ops:
  7.2 37.4 %copy-start = (bf16[512,768]{1,0:T(8,128)(2,1)S(1)}, bf16[512,768]{1,0:T(8,128)(2,1)}, u32[]{:S(2)}) copy-start(bf16[512,768]{1,0:T(8,128)(2,1)} %param.10) | copy-start | bytes 2359300
  7.2 13.7 %copy-start.1 = (bf16[1,32,8,512]{3,2,1,0:T(8,128)(2,1)S(1)}, bf16[1,32,8,512]{3,2,1,0:T(8,128)(2,1)}, u32[]{:S(2)}) copy-start(bf16[1,32,8,512]{3,2,1,0:T(8,128)(2,1)} %param.6) | copy-start | bytes 786436
  7.2 12.3 %copy-start.20 = (f32[7,7,512]{2,1,0:T(8,128)S(1)}, f32[7,7,512]{2,1,0:T(8,128)}, u32[]{:S(2)}) copy-start(f32[7,7,512]{2,1,0:T(8,128)} %param.8) | copy-start | bytes 301060
  8.4 12.4 %collective-permute-start = (bf16[1,32,3,512]{3,2,1,0:T(4,128)(2,1)S(1)}, bf16[1,32,3,512]{3,2,1,0:T(4,128)(2,1)S(1)}, u32[]{:S(2)}, u32[]{:S(2)}) collective-permute-start(bf16[1,32,3,512]{3,2,1,0:T(4,128)(2,1)S(1)} %get-tuple-element.93), channel_id=1, source_target_pairs={{0,4},{4,8},{8,12},{12,0},{1,5},{5,9},{9,13},{13,1},{2,6},{6,10},{... | collective-permute-start | bytes 294920 | tf_op jit(solution)/shard_map/ppermute | solution.py:20
  11.6 9.3 %collective-permute-start.1 = (bf16[1,32,3,512]{3,2,1,0:T(4,128)(2,1)S(1)}, bf16[1,32,3,512]{3,2,1,0:T(4,128)(2,1)S(1)}, u32[]{:S(2)}, u32[]{:S(2)}) collective-permute-start(bf16[1,32,3,512]{3,2,1,0:T(4,128)(2,1)S(1)} %get-tuple-element.94), channel_id=1, source_target_pairs={{4,0},{8,4},{12,8},{0,12},{5,1},{9,5},{13,9},{1,13},{6,2},{10,6},{... | collective-permute-start | bytes 294920 | tf_op jit(solution)/shard_map/ppermute | solution.py:21
  15.6 30.2 %all-to-all-start.2 = ((bf16[1,32,8,256]{3,2,0,1:T(8,128)(2,1)}), bf16[1,32,8,256]{3,2,0,1:T(8,128)(2,1)}, u32[]{:S(2)}, u32[]{:S(2)}) async-start(bf16[1,32,8,256]{3,2,0,1:T(8,128)(2,1)} %fusion.15), calls=%async_computation.2 | async-start | bytes 262144 | tf_op jit(solution)/shard_map/all_to_all | solution.py:142
  20.8 11.2 %copy-start.8 = (bf16[1,32,3,512]{3,2,1,0:T(4,128)(2,1)}, bf16[1,32,3,512]{3,2,1,0:T(4,128)(2,1)S(1)}, u32[]{:S(2)}) copy-start(bf16[1,32,3,512]{3,2,1,0:T(4,128)(2,1)S(1)} %collective-permute-done) | copy-start | bytes 294916
  20.9 11.1 %copy-start.10 = (bf16[1,32,3,512]{3,2,1,0:T(4,128)(2,1)}, bf16[1,32,3,512]{3,2,1,0:T(4,128)(2,1)S(1)}, u32[]{:S(2)}) copy-start(bf16[1,32,3,512]{3,2,1,0:T(4,128)(2,1)S(1)} %collective-permute-done.1) | copy-start | bytes 294916
  22.1 5.5 %collective-permute-start.2 = (bf16[1,3,14,512]{3,2,1,0:T(8,128)(2,1)S(1)}, bf16[1,3,14,512]{3,2,1,0:T(8,128)(2,1)S(1)}, u32[]{:S(2)}, u32[]{:S(2)}) collective-permute-start(bf16[1,3,14,512]{3,2,1,0:T(8,128)(2,1)S(1)} %get-tuple-element.84), channel_id=1, source_target_pairs={{0,2},{1,3},{4,6},{5,7},{8,10},{9,11},{12,14},{13,15},{16,18},{17,... | collective-permute-start | bytes 129032 | tf_op jit(solution)/shard_map/ppermute | solution.py:20
  25.7 6.0 %collective-permute-start.3 = (bf16[1,3,14,512]{3,2,1,0:T(8,128)(2,1)S(1)}, bf16[1,3,14,512]{3,2,1,0:T(8,128)(2,1)S(1)}, u32[]{:S(2)}, u32[]{:S(2)}) collective-permute-start(bf16[1,3,14,512]{3,2,1,0:T(8,128)(2,1)S(1)} %get-tuple-element.85), channel_id=1, source_target_pairs={{2,0},{3,1},{6,4},{7,5},{10,8},{11,9},{14,12},{15,13},{18,16},{19,... | collective-permute-start | bytes 129032 | tf_op jit(solution)/shard_map/ppermute | solution.py:21
  34.0 10.5 %copy-start.21 = (f32[512]{0:T(512)S(1)}, f32[512]{0:T(512)}, u32[]{:S(2)}) copy-start(f32[512]{0:T(512)} %param.9) | copy-start | bytes 6148
  44.5 6.2 %copy-start.2 = (bf16[1,32,8,512]{3,2,1,0:T(8,128)(2,1)S(1)}, bf16[1,32,8,512]{3,2,1,0:T(8,128)(2,1)}, u32[]{:S(2)}) copy-start(bf16[1,32,8,512]{3,2,1,0:T(8,128)(2,1)} %param.6) | copy-start | bytes 786436
  45.7 14.6 %all-to-all-start = ((bf16[1,32,8,768]{3,2,0,1:T(8,128)(2,1)}), bf16[1,32,8,768]{3,2,0,1:T(8,128)(2,1)S(1)}, u32[]{:S(2)}, u32[]{:S(2)}) async-start(bf16[1,32,8,768]{3,2,0,1:T(8,128)(2,1)} %fusion.10), calls=%async_computation | async-start | bytes 786432 | tf_op jit(solution)/shard_map/all_to_all | solution.py:125
  71.2 7.9 %copy-start.17 = (bf16[8,32,4,64]{3,2,1,0:T(4,128)(2,1)S(1)}, bf16[8,32,4,64]{3,2,1,0:T(4,128)(2,1)}, u32[]{:S(2)}) copy-start(bf16[8,32,4,64]{3,2,1,0:T(4,128)(2,1)} %reshape.608) | copy-start | bytes 393220
  75.1 12.5 %all-to-all-start.1 = ((bf16[1,8,32,256]{3,1,0,2:T(8,128)(2,1)}), bf16[1,8,32,256]{3,1,0,2:T(8,128)(2,1)}, u32[]{:S(2)}, u32[]{:S(2)}) async-start(bf16[1,8,32,256]{3,1,0,2:T(8,128)(2,1)} %reshape.619), calls=%async_computation.1 | async-start | bytes 262144 | tf_op jit(solution)/shard_map/all_to_all | solution.py:133
  86.7 8.6 %copy-start.5 = (bf16[1,32,8,512]{3,2,1,0:T(8,128)(2,1)S(1)}, bf16[1,32,8,512]{3,2,1,0:T(8,128)(2,1)}, u32[]{:S(2)}) copy-start(bf16[1,32,8,512]{3,2,1,0:T(8,128)(2,1)} %param.7) | copy-start | bytes 786436
  87.6 13.9 %all-to-all-start.3 = ((bf16[1,8,32,768]{3,1,0,2:T(8,128)(2,1)}), bf16[1,8,32,768]{3,1,0,2:T(8,128)(2,1)S(1)}, u32[]{:S(2)}, u32[]{:S(2)}) async-start(bf16[1,8,32,768]{3,1,0,2:T(8,128)(2,1)} %copy.93), calls=%async_computation.3 | async-start | bytes 786432 | tf_op jit(solution)/shard_map/all_to_all | solution.py:150
  92.7 129.4 %all-reduce.3.cloned.1.call-start = ((), (), s32[]{:S(2)}) async-start(), calls=%async_computation.4 | async-start | bytes 4423680 | tf_op jit(solution)/shard_map/psum | solution.py:173
  104.9 6.0 %copy-start.7 = (bf16[1,32,11,512]{3,2,1,0:T(8,128)(2,1)S(1)}, bf16[1,32,11,512]{3,2,1,0:T(8,128)(2,1)}, u32[]{:S(2)}) copy-start(bf16[1,32,11,512]{3,2,1,0:T(8,128)(2,1)} %constant_dynamic-update-slice_fusion) | copy-start | bytes 1081348
  104.9 6.0 %copy-start.9 = (bf16[1,32,3,512]{3,2,1,0:T(4,128)(2,1)S(1)}, bf16[1,32,3,512]{3,2,1,0:T(4,128)(2,1)}, u32[]{:S(2)}) copy-start(bf16[1,32,3,512]{3,2,1,0:T(4,128)(2,1)} %copy-done.8) | copy-start | bytes 294916
  106.9 7.1 %copy-start.3 = (bf16[1,32,8,512]{3,2,1,0:T(8,128)(2,1)}, bf16[1,32,8,512]{3,2,1,0:T(8,128)(2,1)S(1)}, u32[]{:S(2)}) copy-start(bf16[1,32,8,512]{3,2,1,0:T(8,128)(2,1)S(1)} %get-tuple-element.79) | copy-start | bytes 786436
  107.0 6.9 %collective-permute-start.4 = (bf16[1,32,3,512]{3,2,1,0:T(4,128)(2,1)S(1)}, bf16[1,32,3,512]{3,2,1,0:T(4,128)(2,1)S(1)}, u32[]{:S(2)}, u32[]{:S(2)}) collective-permute-start(bf16[1,32,3,512]{3,2,1,0:T(4,128)(2,1)S(1)} %get-tuple-element.91), channel_id=1, source_target_pairs={{0,4},{4,8},{8,12},{12,0},{1,5},{5,9},{9,13},{13,1},{2,6},{6,10},{... | collective-permute-start | bytes 294920 | tf_op jit(solution)/shard_map/ppermute | solution.py:20
  107.6 6.4 %collective-permute-start.5 = (bf16[1,32,3,512]{3,2,1,0:T(4,128)(2,1)S(1)}, bf16[1,32,3,512]{3,2,1,0:T(4,128)(2,1)S(1)}, u32[]{:S(2)}, u32[]{:S(2)}) collective-permute-start(bf16[1,32,3,512]{3,2,1,0:T(4,128)(2,1)S(1)} %get-tuple-element.92), channel_id=1, source_target_pairs={{4,0},{8,4},{12,8},{0,12},{5,1},{9,5},{13,9},{1,13},{6,2},{10,6},{... | collective-permute-start | bytes 294920 | tf_op jit(solution)/shard_map/ppermute | solution.py:21
  114.1 38.6 %collective-permute-start.6 = (bf16[1,3,14,512]{3,2,1,0:T(8,128)(2,1)S(1)}, bf16[1,3,14,512]{3,2,1,0:T(8,128)(2,1)S(1)}, u32[]{:S(2)}, u32[]{:S(2)}) collective-permute-start(bf16[1,3,14,512]{3,2,1,0:T(8,128)(2,1)S(1)} %get-tuple-element.80), channel_id=1, source_target_pairs={{0,2},{1,3},{4,6},{5,7},{8,10},{9,11},{12,14},{13,15},{16,18},{17,... | collective-permute-start | bytes 129032 | tf_op jit(solution)/shard_map/ppermute | solution.py:20
  116.3 36.4 %collective-permute-start.7 = (bf16[1,3,14,512]{3,2,1,0:T(8,128)(2,1)S(1)}, bf16[1,3,14,512]{3,2,1,0:T(8,128)(2,1)S(1)}, u32[]{:S(2)}, u32[]{:S(2)}) collective-permute-start(bf16[1,3,14,512]{3,2,1,0:T(8,128)(2,1)S(1)} %get-tuple-element.81), channel_id=1, source_target_pairs={{2,0},{3,1},{6,4},{7,5},{10,8},{11,9},{14,12},{15,13},{18,16},{19,... | collective-permute-start | bytes 129032 | tf_op jit(solution)/shard_map/ppermute | solution.py:21
  119.8 32.8 %copy-start.4 = (bf16[1,32,8,512]{3,2,1,0:T(8,128)(2,1)S(1)}, bf16[1,32,8,512]{3,2,1,0:T(8,128)(2,1)}, u32[]{:S(2)}) copy-start(bf16[1,32,8,512]{3,2,1,0:T(8,128)(2,1)} %copy-done.3) | copy-start | bytes 786436
  119.8 32.8 %copy-start.13 = (bf16[1,32,3,512]{3,2,1,0:T(4,128)(2,1)S(1)}, bf16[1,32,3,512]{3,2,1,0:T(4,128)(2,1)}, u32[]{:S(2)}) copy-start(bf16[1,32,3,512]{3,2,1,0:T(4,128)(2,1)} %copy-done.12) | copy-start | bytes 294916
  119.8 32.8 %copy-start.15 = (bf16[1,32,3,512]{3,2,1,0:T(4,128)(2,1)S(1)}, bf16[1,32,3,512]{3,2,1,0:T(4,128)(2,1)}, u32[]{:S(2)}) copy-start(bf16[1,32,3,512]{3,2,1,0:T(4,128)(2,1)} %copy-done.14) | copy-start | bytes 294916
  120.5 32.4 %copy-start.22 = (f32[1,1,512]{2,1,0:T(1,128)S(1)}, f32[1,1,512]{2,1,0:T(1,128)}, u32[]{:S(2)}) copy-start(f32[1,1,512]{2,1,0:T(1,128)} %get-tuple-element.108) | copy-start | bytes 6148
  120.6 32.4 %copy-start.23 = (f32[1,1,512]{2,1,0:T(1,128)S(1)}, f32[1,1,512]{2,1,0:T(1,128)}, u32[]{:S(2)}) copy-start(f32[1,1,512]{2,1,0:T(1,128)} %get-tuple-element.109) | copy-start | bytes 6148
  120.6 32.4 %copy-start.24 = (f32[1,1,512]{2,1,0:T(1,128)S(1)}, f32[1,1,512]{2,1,0:T(1,128)}, u32[]{:S(2)}) copy-start(f32[1,1,512]{2,1,0:T(1,128)} %get-tuple-element.110) | copy-start | bytes 6148
  120.6 32.4 %copy-start.25 = (f32[1,1,512]{2,1,0:T(1,128)S(1)}, f32[1,1,512]{2,1,0:T(1,128)}, u32[]{:S(2)}) copy-start(f32[1,1,512]{2,1,0:T(1,128)} %get-tuple-element.111) | copy-start | bytes 6148
  120.6 32.4 %copy-start.26 = (f32[1,1,512]{2,1,0:T(1,128)S(1)}, f32[1,1,512]{2,1,0:T(1,128)}, u32[]{:S(2)}) copy-start(f32[1,1,512]{2,1,0:T(1,128)} %get-tuple-element.112) | copy-start | bytes 6148
  120.6 32.4 %copy-start.27 = (f32[1,1,512]{2,1,0:T(1,128)S(1)}, f32[1,1,512]{2,1,0:T(1,128)}, u32[]{:S(2)}) copy-start(f32[1,1,512]{2,1,0:T(1,128)} %get-tuple-element.113) | copy-start | bytes 6148
  120.6 32.4 %copy-start.28 = (f32[1,1,512]{2,1,0:T(1,128)S(1)}, f32[1,1,512]{2,1,0:T(1,128)}, u32[]{:S(2)}) copy-start(f32[1,1,512]{2,1,0:T(1,128)} %get-tuple-element.114) | copy-start | bytes 6148
  120.6 32.4 %copy-start.29 = (f32[1,1,512]{2,1,0:T(1,128)S(1)}, f32[1,1,512]{2,1,0:T(1,128)}, u32[]{:S(2)}) copy-start(f32[1,1,512]{2,1,0:T(1,128)} %get-tuple-element.115) | copy-start | bytes 6148
  120.6 32.4 %copy-start.30 = (f32[1,1,512]{2,1,0:T(1,128)S(1)}, f32[1,1,512]{2,1,0:T(1,128)}, u32[]{:S(2)}) copy-start(f32[1,1,512]{2,1,0:T(1,128)} %get-tuple-element.116) | copy-start | bytes 6148
  120.6 32.4 %copy-start.31 = (f32[1,1,512]{2,1,0:T(1,128)S(1)}, f32[1,1,512]{2,1,0:T(1,128)}, u32[]{:S(2)}) copy-start(f32[1,1,512]{2,1,0:T(1,128)} %get-tuple-element.117) | copy-start | bytes 6148
  120.6 32.4 %copy-start.32 = (f32[1,1,512]{2,1,0:T(1,128)S(1)}, f32[1,1,512]{2,1,0:T(1,128)}, u32[]{:S(2)}) copy-start(f32[1,1,512]{2,1,0:T(1,128)} %get-tuple-element.118) | copy-start | bytes 6148
  120.7 32.4 %copy-start.33 = (f32[1,1,512]{2,1,0:T(1,128)S(1)}, f32[1,1,512]{2,1,0:T(1,128)}, u32[]{:S(2)}) copy-start(f32[1,1,512]{2,1,0:T(1,128)} %get-tuple-element.119) | copy-start | bytes 6148
  120.7 32.4 %copy-start.34 = (f32[1,1,512]{2,1,0:T(1,128)S(1)}, f32[1,1,512]{2,1,0:T(1,128)}, u32[]{:S(2)}) copy-start(f32[1,1,512]{2,1,0:T(1,128)} %get-tuple-element.120) | copy-start | bytes 6148
  120.7 32.4 %copy-start.35 = (f32[1,1,512]{2,1,0:T(1,128)S(1)}, f32[1,1,512]{2,1,0:T(1,128)}, u32[]{:S(2)}) copy-start(f32[1,1,512]{2,1,0:T(1,128)} %get-tuple-element.121) | copy-start | bytes 6148
  120.7 32.4 %copy-start.36 = (f32[1,1,512]{2,1,0:T(1,128)S(1)}, f32[1,1,512]{2,1,0:T(1,128)}, u32[]{:S(2)}) copy-start(f32[1,1,512]{2,1,0:T(1,128)} %get-tuple-element.122) | copy-start | bytes 6148
  120.7 32.4 %copy-start.37 = (f32[1,1,512]{2,1,0:T(1,128)S(1)}, f32[1,1,512]{2,1,0:T(1,128)}, u32[]{:S(2)}) copy-start(f32[1,1,512]{2,1,0:T(1,128)} %get-tuple-element.123) | copy-start | bytes 6148
  120.7 32.4 %copy-start.38 = (f32[1,1,512]{2,1,0:T(1,128)S(1)}, f32[1,1,512]{2,1,0:T(1,128)}, u32[]{:S(2)}) copy-start(f32[1,1,512]{2,1,0:T(1,128)} %get-tuple-element.124) | copy-start | bytes 6148
  120.7 32.4 %copy-start.39 = (f32[1,1,512]{2,1,0:T(1,128)S(1)}, f32[1,1,512]{2,1,0:T(1,128)}, u32[]{:S(2)}) copy-start(f32[1,1,512]{2,1,0:T(1,128)} %get-tuple-element.125) | copy-start | bytes 6148
  120.7 32.4 %copy-start.40 = (f32[1,1,512]{2,1,0:T(1,128)S(1)}, f32[1,1,512]{2,1,0:T(1,128)}, u32[]{:S(2)}) copy-start(f32[1,1,512]{2,1,0:T(1,128)} %get-tuple-element.126) | copy-start | bytes 6148
  120.7 32.4 %copy-start.41 = (f32[1,1,512]{2,1,0:T(1,128)S(1)}, f32[1,1,512]{2,1,0:T(1,128)}, u32[]{:S(2)}) copy-start(f32[1,1,512]{2,1,0:T(1,128)} %get-tuple-element.127) | copy-start | bytes 6148
  120.7 32.4 %copy-start.42 = (f32[1,1,512]{2,1,0:T(1,128)S(1)}, f32[1,1,512]{2,1,0:T(1,128)}, u32[]{:S(2)}) copy-start(f32[1,1,512]{2,1,0:T(1,128)} %get-tuple-element.128) | copy-start | bytes 6148
  120.8 32.4 %copy-start.43 = (f32[1,1,512]{2,1,0:T(1,128)S(1)}, f32[1,1,512]{2,1,0:T(1,128)}, u32[]{:S(2)}) copy-start(f32[1,1,512]{2,1,0:T(1,128)} %get-tuple-element.129) | copy-start | bytes 6148
  120.8 32.4 %copy-start.44 = (f32[1,1,512]{2,1,0:T(1,128)S(1)}, f32[1,1,512]{2,1,0:T(1,128)}, u32[]{:S(2)}) copy-start(f32[1,1,512]{2,1,0:T(1,128)} %get-tuple-element.130) | copy-start | bytes 6148
  120.8 32.4 %copy-start.45 = (f32[1,1,512]{2,1,0:T(1,128)S(1)}, f32[1,1,512]{2,1,0:T(1,128)}, u32[]{:S(2)}) copy-start(f32[1,1,512]{2,1,0:T(1,128)} %get-tuple-element.131) | copy-start | bytes 6148
  120.8 32.4 %copy-start.46 = (f32[1,1,512]{2,1,0:T(1,128)S(1)}, f32[1,1,512]{2,1,0:T(1,128)}, u32[]{:S(2)}) copy-start(f32[1,1,512]{2,1,0:T(1,128)} %get-tuple-element.132) | copy-start | bytes 6148
  120.8 32.4 %copy-start.47 = (f32[1,1,512]{2,1,0:T(1,128)S(1)}, f32[1,1,512]{2,1,0:T(1,128)}, u32[]{:S(2)}) copy-start(f32[1,1,512]{2,1,0:T(1,128)} %get-tuple-element.133) | copy-start | bytes 6148
  120.8 32.4 %copy-start.48 = (f32[1,1,512]{2,1,0:T(1,128)S(1)}, f32[1,1,512]{2,1,0:T(1,128)}, u32[]{:S(2)}) copy-start(f32[1,1,512]{2,1,0:T(1,128)} %get-tuple-element.134) | copy-start | bytes 6148
  120.8 32.4 %copy-start.49 = (f32[1,1,512]{2,1,0:T(1,128)S(1)}, f32[1,1,512]{2,1,0:T(1,128)}, u32[]{:S(2)}) copy-start(f32[1,1,512]{2,1,0:T(1,128)} %get-tuple-element.135) | copy-start | bytes 6148
  120.8 32.4 %copy-start.50 = (f32[1,1,512]{2,1,0:T(1,128)S(1)}, f32[1,1,512]{2,1,0:T(1,128)}, u32[]{:S(2)}) copy-start(f32[1,1,512]{2,1,0:T(1,128)} %get-tuple-element.136) | copy-start | bytes 6148
  120.8 32.4 %copy-start.51 = (f32[1,1,512]{2,1,0:T(1,128)S(1)}, f32[1,1,512]{2,1,0:T(1,128)}, u32[]{:S(2)}) copy-start(f32[1,1,512]{2,1,0:T(1,128)} %get-tuple-element.137) | copy-start | bytes 6148
  120.8 32.4 %copy-start.52 = (f32[1,1,512]{2,1,0:T(1,128)S(1)}, f32[1,1,512]{2,1,0:T(1,128)}, u32[]{:S(2)}) copy-start(f32[1,1,512]{2,1,0:T(1,128)} %get-tuple-element.138) | copy-start | bytes 6148
  120.9 32.4 %copy-start.53 = (f32[1,1,512]{2,1,0:T(1,128)S(1)}, f32[1,1,512]{2,1,0:T(1,128)}, u32[]{:S(2)}) copy-start(f32[1,1,512]{2,1,0:T(1,128)} %get-tuple-element.139) | copy-start | bytes 6148
  120.9 32.4 %copy-start.54 = (f32[1,1,512]{2,1,0:T(1,128)S(1)}, f32[1,1,512]{2,1,0:T(1,128)}, u32[]{:S(2)}) copy-start(f32[1,1,512]{2,1,0:T(1,128)} %get-tuple-element.140) | copy-start | bytes 6148
  120.9 32.4 %copy-start.55 = (f32[1,1,512]{2,1,0:T(1,128)S(1)}, f32[1,1,512]{2,1,0:T(1,128)}, u32[]{:S(2)}) copy-start(f32[1,1,512]{2,1,0:T(1,128)} %get-tuple-element.141) | copy-start | bytes 6148
  120.9 32.4 %copy-start.56 = (f32[1,1,512]{2,1,0:T(1,128)S(1)}, f32[1,1,512]{2,1,0:T(1,128)}, u32[]{:S(2)}) copy-start(f32[1,1,512]{2,1,0:T(1,128)} %get-tuple-element.142) | copy-start | bytes 6148
  120.9 32.4 %copy-start.57 = (f32[1,1,512]{2,1,0:T(1,128)S(1)}, f32[1,1,512]{2,1,0:T(1,128)}, u32[]{:S(2)}) copy-start(f32[1,1,512]{2,1,0:T(1,128)} %get-tuple-element.143) | copy-start | bytes 6148
  (44 other events, 140.4 us)
Sparse Core Ops, SparseCore 0:
  120.7 101.3 all-reduce.2
where the time goes:
time: 234 us; the launch traced here: 233 us
  waiting for transfers between devices  80.2 us (34%)
  starting transfers between devices  35 us (15%)
  blocking collectives  31.5 us (13%)
  local copies, waits for them, and re-layouts  25.9 us (11%)
  other arithmetic  25.8 us (11%)
  matrix products  19.2 us (8%)
  between operations  15.5 us (7%)
    psum x1, waiting for transfers between devices, on_device(): lax.psum((grad_weight, grad_out, grad_conv, grad_gain), ('lon', 'lat', 'd...  64.3 us
    psum x1, blocking collectives, on_device(): lax.psum((grad_weight, grad_out, grad_conv, grad_gain), ('lon', 'lat', 'd...  31.5 us
    reduce_sum x1, other arithmetic, on_device(): inverse = lax.rsqrt(jnp.mean(update * update, -1, keepdims=True) + EPSILON)  10.5 us
    ppermute x4, starting transfers between devices, with_halo(): before = lax.ppermute(last, axis, up)  9.14 us
    ppermute x4, starting transfers between devices, with_halo(): after = lax.ppermute(first, axis, down)  7.95 us
    all_to_all x1, waiting for transfers between devices, on_device(): lax.all_to_all(projected.reshape(batch_count, lat_rows, lon_cols, 3 * att...  6.17 us
    reduce_sum x3, other arithmetic, correlate(): pieces.append(jnp.sum(window * upstream, axis=(0, 1, 2)))  5.91 us
    unnamed x194, local copies, waits for them, and re-layouts  5.57 us
  transfers between devices with their start and end apart: 13, of which 6 were waited for; matrix products, arithmetic and copies ran while one was open for 19% of the time, Pallas kernels for 0%

commit v1 on v0

--- a/solution.py
+++ b/solution.py
@@ -1,6 +1,11 @@
+import functools
+import itertools
+
 import jax
 import jax.numpy as jnp
 from jax import lax
+from jax.experimental import pallas as pl
+from jax.experimental.pallas import tpu as pltpu
 from jax.sharding import PartitionSpec as P
 
 HEADS = 4
@@ -112,7 +117,7 @@
     )
 
 
-def on_device(fields, cotangent, conv_weight, norm_gain, w_qkv, w_out):
+def on_device_native(fields, cotangent, conv_weight, norm_gain, w_qkv, w_out):
     batch_count, lat_rows, lon_cols, channels = fields.shape
     att_width = w_out.shape[0]
     wide = with_halo(fields, (("lon", 2),), 3, True)
@@ -174,6 +179,564 @@
     return (result, grad_fields, totals[0], totals[1], totals[2], totals[3])
 
 
+MESH = pl.DeviceIdType.MESH
+AXES = ("lat", "lon", "dp")
+LANES = 128
+
+
+def place():
+    return tuple(lax.axis_index(a) for a in AXES)
+
+
+def greet(sizes):
+    me = place()
+    barrier = pltpu.get_barrier_semaphore()
+    count = 0
+    for offset in itertools.product(*(range(s) for s in sizes)):
+        if not any(offset):
+            continue
+        target = {a: lax.rem(m + o, s) for a, m, o, s in zip(AXES, me, offset, sizes)}
+        pl.semaphore_signal(barrier, inc=1, device_id=target, device_id_type=MESH)
+        count += 1
+    pl.semaphore_wait(barrier, count)
+
+
+def remote(src, dst, send, recv, target):
+    return pltpu.make_async_remote_copy(
+        src_ref=src, dst_ref=dst, send_sem=send, recv_sem=recv, device_id=target, device_id_type=MESH
+    )
+
+
+def bring_rows(sizes, f_ref, c_ref, fp_ref, cr_ref, send, recv, xsend, xrecv):
+    n_lat, n_lon, _ = sizes
+    lat, lon, _ = place()
+    rows = f_ref.shape[0]
+    own = rows // n_lon
+
+    def fields_copy(i, j):
+        low, high = max(0, own * j - 3), min(rows, own * j + own + 3)
+        start = low - (own * j - 3)
+        return remote(
+            f_ref.at[low:high],
+            fp_ref.at[start : start + high - low, i],
+            send.at[0, j],
+            recv.at[0, i],
+            {"lon": j},
+        )
+
+    def cot_copy(i, j):
+        return remote(
+            c_ref.at[own * j : own * j + own], cr_ref.at[:, i], send.at[1, j], recv.at[1, i], {"lon": j}
+        )
+
+    def below(i):
+        return remote(
+            f_ref.at[rows - 3 : rows], fp_ref.at[0:3, i], xsend.at[0], xrecv.at[0, i],
+            {"lat": lat + 1, "lon": 0},
+        )
+
+    def above(i):
+        return remote(
+            f_ref.at[0:3], fp_ref.at[own + 3 : own + 6, i], xsend.at[1], xrecv.at[1, i],
+            {"lat": lat - 1, "lon": n_lon - 1},
+        )
+
+    greet(sizes)
+
+    @pl.when(lat < n_lat - 1)
+    def _():
+        below(lon).start()
+
+    @pl.when(lat > 0)
+    def _():
+        above(lon).start()
+
+    for j in range(n_lon):
+
+        @pl.when(lon != j)
+        def _(j=j):
+            fields_copy(lon, j).start()
+
+    for j in range(n_lon):
+
+        @pl.when(lon != j)
+        def _(j=j):
+            cot_copy(lon, j).start()
+
+        @pl.when(lon == j)
+        def _(j=j):
+            low, high = max(0, own * j - 3), min(rows, own * j + own + 3)
+            start = low - (own * j - 3)
+            fp_ref[start : start + high - low, j] = f_ref[low:high]
+            cr_ref[:, j] = c_ref[own * j : own * j + own]
+
+    @pl.when((lat == 0) & (lon == 0))
+    def _():
+        fp_ref[0:3] = jnp.zeros((3,) + fp_ref.shape[1:], fp_ref.dtype)
+
+    @pl.when((lat == n_lat - 1) & (lon == n_lon - 1))
+    def _():
+        fp_ref[own + 3 : own + 6] = jnp.zeros((3,) + fp_ref.shape[1:], fp_ref.dtype)
+
+    for j in range(n_lon):
+
+        @pl.when(lon == j)
+        def _(j=j):
+            for i in range(n_lon):
+                if i != j:
+                    fields_copy(i, j).wait_recv()
+                    cot_copy(i, j).wait_recv()
+
+        @pl.when(lon != j)
+        def _(j=j):
+            fields_copy(lon, j).wait_send()
+            cot_copy(lon, j).wait_send()
+
+    @pl.when((lat > 0) & (lon == 0))
+    def _():
+        for i in range(n_lon):
+            below(i).wait_recv()
+
+    @pl.when((lat < n_lat - 1) & (lon == n_lon - 1))
+    def _():
+        for i in range(n_lon):
+            above(i).wait_recv()
+
+    @pl.when(lat < n_lat - 1)
+    def _():
+        below(lon).wait_send()
+
+    @pl.when(lat > 0)
+    def _():
+        above(lon).wait_send()
+
+
+def convolve(pad, weight, out, own, flip):
+    circle, channels = pad.shape[1], pad.shape[2]
+    for c in range(channels // LANES):
+        lanes = slice(c * LANES, (c + 1) * LANES)
+
+        def row(r, carry, lanes=lanes):
+            bands = [pad[r + a, :, lanes] for a in range(7)]
+            total = bands[3]
+            for e in range(7):
+                part = None
+                for a in range(7):
+                    tap = weight[(6 - a if flip else a) * 7 + e, :, lanes]
+                    term = bands[a] * tap
+                    part = term if part is None else part + term
+                turn = (e - 3 if flip else 3 - e) % circle
+                if turn:
+                    part = pltpu.roll(part, turn, 0)
+                total = total + part
+            out[r, :, lanes] = total
+            return carry
+
+        lax.fori_loop(0, own, row, 0)
+
+
+def correlate_rows(pad, upstream, out, own):
+    circle, channels = pad.shape[1], pad.shape[2]
+
+    def chunk(c, carry):
+        lanes = pl.ds(pl.multiple_of(c * LANES, LANES), LANES)
+        for e in range(7):
+            turn = (e - 3) % circle
+            turned = [upstream[r, :, lanes] for r in range(own)]
+            if turn:
+                turned = [pltpu.roll(t, turn, 0) for t in turned]
+            for a in range(7):
+                total = None
+                for r in range(own):
+                    term = pad[r + a, :, lanes] * turned[r]
+                    total = term if total is None else total + term
+                out[a * 7 + e, :, lanes] = jnp.sum(total, axis=0, keepdims=True)
+        return carry
+
+    lax.fori_loop(0, channels // LANES, chunk, 0)
+
+
+def dot(left, right, dims):
+    return lax.dot_general(left, right, (dims, ((), ())), preferred_element_type=jnp.float32)
+
+
+PLAIN, COLS, ROWS = ((1,), (0,)), ((1,), (1,)), ((0,), (0,))
+
+
+def attend_rows(projected, grad_mixed, circle, att_width):
+    cells = projected.shape[0]
+    group = max(circle, LANES)
+    row_of = lax.broadcasted_iota(jnp.int32, (group, group), 0) // circle
+    col_of = lax.broadcasted_iota(jnp.int32, (group, group), 1) // circle
+    same = row_of == col_of
+    lane_head = lax.broadcasted_iota(jnp.int32, (group, LANES), 1) // HEAD_DIM
+    bf16 = jnp.bfloat16
+    mixed, grads = [], []
+    for g in range(cells // group):
+        cut = slice(g * group, (g + 1) * group)
+        mixed_row, grad_q, grad_k, grad_v = [], [], [], []
+        for pair in range(att_width // LANES):
+            at = slice(pair * LANES, (pair + 1) * LANES)
+            q = projected[cut, :att_width][:, at]
+            k = projected[cut, att_width : 2 * att_width][:, at]
+            v = projected[cut, 2 * att_width :][:, at]
+            up = grad_mixed[cut, at]
+            parts = [[], [], [], []]
+            for h in range(LANES // HEAD_DIM):
+                mine = lane_head == h
+                zero = jnp.zeros((), bf16)
+                scores = dot(jnp.where(mine, q, zero), k, COLS) * HEAD_DIM ** (-0.5)
+                scores = jnp.where(same, scores, -jnp.inf)
+                raised = jnp.exp(scores - jnp.max(scores, -1, keepdims=True))
+                probs = raised / jnp.sum(raised, -1, keepdims=True)
+                weights = probs.astype(bf16)
+                grad_probs = dot(jnp.where(mine, up, zero), v, COLS)
+                inner = jnp.sum(probs * grad_probs, -1, keepdims=True)
+                grad_scores = (probs * (grad_probs - inner) * HEAD_DIM ** (-0.5)).astype(bf16)
+                parts[0].append(dot(weights, v, PLAIN))
+                parts[1].append(dot(grad_scores, k, PLAIN))
+                parts[2].append(dot(grad_scores, q, ROWS))
+                parts[3].append(dot(weights, up, ROWS))
+            for part, found in zip(parts, (mixed_row, grad_q, grad_k, grad_v)):
+                whole = part[0]
+                for h in range(1, len(part)):
+                    whole = jnp.where(lane_head == h, part[h], whole)
+                found.append(whole.astype(bf16))
+        mixed.append(jnp.concatenate(mixed_row, axis=1))
+        grads.append(jnp.concatenate(grad_q + grad_k + grad_v, axis=1))
+    return jnp.concatenate(mixed, axis=0), jnp.concatenate(grads, axis=0)
+
+
+def core_step(fp_ref, cr_ref, weight, gain_ref, wq_ref, wo_ref,
+              result_ref, gu_ref, gub_ref, gq_ref, go_ref, gg_ref, pad, update_ref):
+    own, blocks, width, channels = cr_ref.shape
+    circle, cells = blocks * width, own * blocks * width
+    att_width = wo_ref.shape[0]
+    pad[...] = fp_ref[...].astype(jnp.float32).reshape(pad.shape)
+    convolve(pad, weight, update_ref, own, False)
+    update = update_ref[...].reshape(cells, channels)
+    gain = gain_ref[...]
+    inverse = lax.rsqrt(jnp.mean(update * update, -1, keepdims=True) + EPSILON)
+    normed = (update * inverse * gain).astype(jnp.bfloat16)
+    projected = dot(normed, wq_ref[...], PLAIN).astype(jnp.bfloat16)
+    cot32 = cr_ref[...].astype(jnp.float32).reshape(cells, channels)
+    cot = cot32.astype(jnp.bfloat16)
+    grad_mixed = dot(cot, wo_ref[...], COLS).astype(jnp.bfloat16)
+    mixed, grad_projected = attend_rows(projected, grad_mixed, circle, att_width)
+    result = update + dot(mixed, wo_ref[...], PLAIN)
+    result_ref[...] = result.reshape(result_ref.shape).astype(jnp.bfloat16)
+    go_ref[...] = dot(mixed, cot, ROWS)
+    gq_ref[...] = dot(normed, grad_projected, ROWS)
+    grad_normed = dot(grad_projected, wq_ref[...], COLS)
+    gg_ref[...] = jnp.sum(grad_normed * (update * inverse), axis=0, keepdims=True)
+    gained = gain * grad_normed
+    grad_update = (
+        cot32
+        + inverse * gained
+        - update * (inverse * inverse * inverse) * jnp.mean(gained * update, -1, keepdims=True)
+    )
+    gu_ref[...] = grad_update.reshape(gu_ref.shape)
+    gub_ref[...] = grad_update.reshape(gub_ref.shape).astype(jnp.bfloat16)
+
+
+def halo_rows(sizes, g_ref, top_ref, low_ref, send, recv):
+    n_lat, n_lon, _ = sizes
+    lat, lon, _ = place()
+    own = g_ref.shape[0]
+    index, last = lat * n_lon + lon, n_lat * n_lon - 1
+
+    def at(k):
+        k = lax.rem(k + n_lat * n_lon, n_lat * n_lon)
+        return {"lat": k // n_lon, "lon": lax.rem(k, n_lon)}
+
+    down = remote(g_ref.at[own - 3 : own], top_ref, send.at[0], recv.at[0], at(index + 1))
+    up = remote(g_ref.at[0:3], low_ref, send.at[1], recv.at[1], at(index - 1))
+    greet(sizes)
+
+    @pl.when(index < last)
+    def _():
+        down.start()
+
+    @pl.when(index > 0)
+    def _():
+        up.start()
+
+    @pl.when(index == 0)
+    def _():
+        top_ref[...] = jnp.zeros_like(top_ref)
+
+    @pl.when(index == last)
+    def _():
+        low_ref[...] = jnp.zeros_like(low_ref)
+
+    @pl.when(index > 0)
+    def _():
+        down.wait_recv()
+        up.wait_send()
+
+    @pl.when(index < last)
+    def _():
+        up.wait_recv()
+        down.wait_send()
+
+
+def final_step(fp_ref, gu_ref, top_ref, low_ref, weight, gg_ref, gq_ref, go_ref,
+               gf_ref, big_ref, pad, gpad, out, conv):
+    own, circle, channels = gu_ref.shape
+    pad[...] = fp_ref[...].astype(jnp.float32).reshape(pad.shape)
+    gpad[0:3] = top_ref[...].astype(jnp.float32).reshape((3, circle, channels))
+    gpad[3 : own + 3] = gu_ref[...]
+    gpad[own + 3 :] = low_ref[...].astype(jnp.float32).reshape((3, circle, channels))
+    convolve(gpad, weight, out, own, True)
+    gf_ref[...] = out[...].reshape(gf_ref.shape).astype(jnp.bfloat16)
+    correlate_rows(pad, gu_ref, conv, own)
+    pack(big_ref, gq_ref, go_ref, conv, gg_ref)
+
+
+def pack(big_ref, gq_ref, go_ref, conv, gg_ref):
+    parts, rows, _ = big_ref.shape
+    whole = parts * rows
+    wide = gq_ref.shape[1]
+    att, channels = go_ref.shape
+    bf16 = jnp.bfloat16
+    fold = whole // att
+    part = channels // fold
+    big_ref[:, :, :wide] = gq_ref[...].reshape(parts, rows, wide).astype(bf16)
+    small = jnp.concatenate([conv[k] for k in range(49)] + [gg_ref[...]], axis=0)
+    small = jnp.concatenate([small, jnp.zeros((64 - 50, channels), jnp.float32)], axis=0)
+    for k in range(fold):
+        piece = go_ref[:, k * part : (k + 1) * part].astype(bf16).reshape(parts // fold, rows, part)
+        big_ref[k * (parts // fold) : (k + 1) * (parts // fold), :, wide : wide + part] = piece
+    step = 64 // rows
+    big_ref[:, :, wide + part :] = jnp.zeros((parts, rows, LANES), bf16)
+    for k in range(channels // LANES):
+        piece = small[:, k * LANES : (k + 1) * LANES].astype(bf16).reshape(step, rows, LANES)
+        big_ref[k * step : (k + 1) * step, :, wide + part :] = piece
+
+
+def unpack(big, channels, wide, att):
+    parts, rows, _ = big.shape
+    whole = parts * rows
+    flat = big.reshape(whole, -1).astype(jnp.float32)
+    fold = whole // att
+    part = channels // fold
+    grad_weight = flat[:, :wide]
+    grad_out = jnp.concatenate([flat[k * att : (k + 1) * att, wide : wide + part] for k in range(fold)], axis=1)
+    small = jnp.concatenate(
+        [flat[k * 64 : (k + 1) * 64, wide + part :] for k in range(channels // LANES)], axis=1
+    )
+    return grad_weight, grad_out, small[:49].reshape(7, 7, channels), small[49]
+
+
+def give_rows(n_lon, lon, src, dst, send, recv):
+    own = src.shape[0]
+
+    def copy(i, j):
+        return remote(src.at[:, j], dst.at[pl.ds(i * own, own)], send.at[j], recv.at[i], {"lon": j})
+
+    def start():
+        for j in range(n_lon):
+
+            @pl.when(lon != j)
+            def _(j=j):
+                copy(lon, j).start()
+
+            @pl.when(lon == j)
+            def _(j=j):
+                dst[j * own : (j + 1) * own] = src[:, j]
+
+    def wait():
+        for j in range(n_lon):
+
+            @pl.when(lon == j)
+            def _(j=j):
+                for i in range(n_lon):
+                    if i != j:
+                        copy(i, j).wait_recv()
+
+            @pl.when(lon != j)
+            def _(j=j):
+                copy(lon, j).wait_send()
+
+    return start, wait
+
+
+def sum_stages(sizes, big, all_ref, got1, sum1, got2, sum2, got3, send, recv):
+    n_lat, n_lon, n_dp = sizes
+    lat, lon, dp = place()
+    half, quarter = n_lat * n_lon, n_lon
+    f32 = jnp.float32
+    other_dp, other_lat = 1 - dp, 1 - lat
+    mine = dp * half + lat * quarter
+    one = remote(big.at[pl.ds(other_dp * half, half)], got1, send.at[0], recv.at[0], {"dp": other_dp})
+    two = remote(sum1.at[pl.ds(other_lat * quarter, quarter)], got2, send.at[1], recv.at[1], {"lat": other_lat})
+
+    def three(i, j):
+        return remote(sum2.at[j], got3.at[i], send.at[2 + j], recv.at[2 + i], {"lon": j})
+
+    base = 2 + n_lon
+
+    def four(i, j):
+        spot = all_ref.at[mine + i]
+        return remote(spot, spot, send.at[base + j], recv.at[base + i], {"lon": j})
+
+    base2 = base + n_lon
+
+    def five(side):
+        spot = all_ref.at[pl.ds(dp * half + side * quarter, quarter)]
+        return remote(spot, spot, send.at[base2], recv.at[base2], {"lat": other_lat})
+
+    def six(side):
+        spot = all_ref.at[pl.ds(side * half, half)]
+        return remote(spot, spot, send.at[base2 + 1], recv.at[base2 + 1], {"dp": other_dp})
+
+    def others(do):
+        for j in range(n_lon):
+
+            @pl.when(lon != j)
+            def _(j=j):
+                do(j)
+
+    def s0():
+        one.start()
+
+    def s1():
+        one.wait()
+        for k in range(half):
+            sum1[k] = (big[dp * half + k].astype(f32) + got1[k].astype(f32)).astype(sum1.dtype)
+        two.start()
+
+    def s2():
+        two.wait()
+        for k in range(quarter):
+            sum2[k] = (sum1[lat * quarter + k].astype(f32) + got2[k].astype(f32)).astype(sum2.dtype)
+        others(lambda j: three(lon, j).start())
+        got3[lon] = sum2[lon]
+
+    def s3():
+        others(lambda j: three(j, j).wait_recv())
+        others(lambda j: three(lon, j).wait_send())
+        total = got3[0].astype(f32)
+        for i in range(1, n_lon):
+            total = total + got3[i].astype(f32)
+        all_ref[mine + lon] = total.astype(all_ref.dtype)
+        others(lambda j: four(lon, j).start())
+
+    def s4():
+        others(lambda j: four(j, j).wait_recv())
+        others(lambda j: four(lon, j).wait_send())
+        five(lat).start()
+
+    def s5():
+        five(lat).wait_send()
+        five(other_lat).wait_recv()
+        six(dp).start()
+
+    def s6():
+        six(dp).wait_send()
+        six(other_dp).wait_recv()
+
+    return s0, s1, s2, s3, s4, s5, s6
+
+
+def send_back(sizes, result_ref, gf_ref, big, result_out, gf_out, all_ref,
+              got1, sum1, got2, sum2, got3, send, recv, rsend, rrecv, gsend, grecv):
+    lon = lax.axis_index("lon")
+    stages = sum_stages(sizes, big, all_ref, got1, sum1, got2, sum2, got3, send, recv)
+    start_r, wait_r = give_rows(sizes[1], lon, result_ref, result_out, rsend, rrecv)
+    start_g, wait_g = give_rows(sizes[1], lon, gf_ref, gf_out, gsend, grecv)
+    greet(sizes)
+    stages[0]()
+    start_g()
+    start_r()
+    for stage in stages[1:]:
+        stage()
+    wait_g()
+    wait_r()
+
+
+def call(body, outs, scratch, collective=None):
+    def wrapped(*args):
+        side = {} if collective is None else {"collective_id": collective, "has_side_effects": True}
+        return pl.pallas_call(
+            body,
+            out_shape=outs,
+            in_specs=[pl.BlockSpec(memory_space=pltpu.VMEM)] * len(args),
+            out_specs=[pl.BlockSpec(memory_space=pltpu.VMEM)] * len(outs),
+            scratch_shapes=scratch,
+            compiler_params=pltpu.CompilerParams(vmem_limit_bytes=48 * 2**20, **side),
+        )(*args)
+
+    return wrapped
+
+
+def on_device(sizes, fields, cotangent, conv_weight, norm_gain, w_qkv, w_out):
+    n_lat, n_lon, n_dp = sizes
+    batch, rows, cols, channels = fields.shape
+    own, circle = rows // n_lon, cols * n_lon
+    att = w_out.shape[0]
+    bf16, f32 = jnp.bfloat16, jnp.float32
+    shape = jax.ShapeDtypeStruct
+    sems = pltpu.SemaphoreType.DMA
+    taps = conv_weight.reshape(49, 1, channels)
+    gain = norm_gain.reshape(1, channels)
+    padded, cot = call(
+        functools.partial(bring_rows, sizes),
+        [shape((own + 6, n_lon, cols, channels), bf16), shape((own, n_lon, cols, channels), bf16)],
+        [sems((2, n_lon)), sems((2, n_lon)), sems((2,)), sems((2, n_lon))],
+        1,
+    )(fields[0], cotangent[0])
+    blocked = (own, n_lon, cols, channels)
+    result, gu, gub, gq, go, gg = call(
+        core_step,
+        [shape(blocked, bf16), shape((own, circle, channels), f32), shape(blocked, bf16),
+         shape(w_qkv.shape, f32), shape(w_out.shape, f32), shape((1, channels), f32)],
+        [pltpu.VMEM((own + 6, circle, channels), f32), pltpu.VMEM((own, circle, channels), f32)],
+    )(padded, cot, taps, gain, w_qkv, w_out)
+    top, low = call(
+        functools.partial(halo_rows, sizes),
+        [shape((3,) + blocked[1:], bf16)] * 2,
+        [sems((2,)), sems((2,))],
+        2,
+    )(gub)
+    parts = n_lat * n_lon * n_dp
+    part_rows = channels // parts
+    wide = w_qkv.shape[1] + att * channels // channels + LANES
+    pieces = lambda n: pltpu.VMEM((n, part_rows, wide), bf16)
+    gf, big = call(
+        final_step,
+        [shape(blocked, bf16), shape((parts, part_rows, wide), bf16)],
+        [pltpu.VMEM((own + 6, circle, channels), f32), pltpu.VMEM((own + 6, circle, channels), f32),
+         pltpu.VMEM((own, circle, channels), f32), pltpu.VMEM((49, 1, channels), f32)],
+    )(padded, gu, top, low, taps, gg, gq, go)
+    result, grad_fields, total = call(
+        functools.partial(send_back, sizes),
+        [shape((rows, cols, channels), bf16)] * 2 + [shape((parts, part_rows, wide), bf16)],
+        [pieces(parts // 2), pieces(parts // 2), pieces(n_lon), pieces(n_lon), pieces(n_lon),
+         sems((4 + 2 * n_lon,)), sems((4 + 2 * n_lon,)),
+         sems((n_lon,)), sems((n_lon,)), sems((n_lon,)), sems((n_lon,))],
+        3,
+    )(result, gf, big)
+    grad_weight, grad_out, grad_conv, grad_gain = unpack(total, channels, w_qkv.shape[1], att)
+    return result[None], grad_fields[None], grad_weight, grad_out, grad_conv, grad_gain
+
+
+def pick(mesh, *args):
+    sizes = tuple(mesh.shape[a] for a in AXES)
+    _, rows, cols, channels = args[0].shape
+    att = args[5].shape[0]
+    n_lat, n_lon, n_dp = sizes
+    parts = n_lat * n_lon * n_dp
+    fits = (
+        args[0].shape[0] == 1 and n_lat == 2 and n_dp == 2 and n_lon > 1
+        and rows % n_lon == 0 and rows // n_lon >= 3 and cols % 8 == 0
+        and LANES % (cols * n_lon) == 0 and (rows // n_lon * cols * n_lon) % LANES == 0
+        and channels == 2 * att and channels % (8 * parts) == 0 and 64 % (channels // parts) == 0
+        and att % LANES == 0
+    )
+    return on_device(sizes, *args) if fits else on_device_native(*args)
+
+
 def solution(mesh):
     placed = (
         P(("member", "dp"), "lat", "lon", None),
@@ -184,7 +747,7 @@
         P(),
     )
     return jax.shard_map(
-        on_device,
+        functools.partial(pick, mesh),
         mesh=mesh,
         in_specs=placed,
         out_specs=(

time: 234 us -> 94.3 us (0.40)
  Pallas kernels: 0 us -> 81.2 us
  waiting for transfers between devices: 80.2 us -> 0 us
  starting transfers between devices: 35 us -> 0 us
  blocking collectives: 31.5 us -> 0 us
  other arithmetic: 25.8 us -> 1.71 us
  matrix products: 19.2 us -> 0 us
  local copies, waits for them, and re-layouts: 25.9 us -> 9.04 us
  between operations: 15.5 us -> 0.73 us
    pallas_call x0 -> x5, Pallas kernels: none -> 81.2 us  [wrapped(): pl.pallas_call(body, out_shape=outs, in_specs=[pl.BlockSpec(memory_space=...]
    psum x1 -> x0, waiting for transfers between devices: 64.3 us -> none  [on_device(): lax.psum((grad_weight, grad_out, grad_conv, grad_gain), ('lon', 'lat', 'd...]
    psum x1 -> x0, blocking collectives: 31.5 us -> none  [on_device(): lax.psum((grad_weight, grad_out, grad_conv, grad_gain), ('lon', 'lat', 'd...]
    all_to_all x4 -> x0, starting transfers between devices: 17.9 us -> none  [the longest x1 5.04 us: on_device(): lax.all_to_all(grad_projected_rows, 'lon', split_axis=2, concat_axis=1, t...]
    ppermute x8 -> x0, starting transfers between devices: 17.1 us -> none  [the longest x4 9.14 us: with_halo(): before = lax.ppermute(last, axis, up)]
    dot_general x11 -> x0, matrix products: 17.1 us -> none  [the longest x2 2.97 us: contract_cols(): lax.dot_general(left, right, (((1,), (1,)), ((), ())), preferred_element_...]
    reduce_sum x4 -> x0, other arithmetic: 16.4 us -> none  [the longest x1 10.5 us: on_device(): inverse = lax.rsqrt(jnp.mean(update * update, -1, keepdims=True) + EPSILON)]
    all_to_all x4 -> x0, waiting for transfers between devices: 10.4 us -> none  [the longest x1 6.17 us: on_device(): lax.all_to_all(projected.reshape(batch_count, lat_rows, lon_cols, 3 * att...]
  transfers between devices with their start and end apart: 13 -> 0, of which waited for: 6 -> 0; matrix products, arithmetic and copies ran while one was open for 19% -> 0% of each run, Pallas kernels for 0% -> 0%
where the time goes in v1:
time: 94.3 us; the launch traced here: 92.7 us
  Pallas kernels  81.2 us (86%)
  local copies, waits for them, and re-layouts  9.04 us (10%)
  other arithmetic  1.71 us (2%)
    pallas_call x5, Pallas kernels, wrapped(): pl.pallas_call(body, out_shape=outs, in_specs=[pl.BlockSpec(memory_space=...  81.2 us
    unnamed x12, local copies, waits for them, and re-layouts  6.06 us

profile of v1, /device:TPU:0, one launch (start us, length us, event | category | flops | bytes accessed | tf_op | source)
XLA Modules:
  0.0 92.7 jit_solution(5229736782958622658)
XLA Ops:
  0.6 1.0 %reshape.24.weight = f32[49,1,512]{2,1,0:T(1,128)S(1)} reshape(f32[7,7,512]{2,1,0:T(8,128)} %param.8) | data formatting | bytes 200704 | tf_op jit(solution)/shard_map/reshape | solution.py:681
  1.6 0.0 copy-start.2
  1.7 0.9 %copy-done.2 = bf16[1,32,8,512]{3,2,1,0:T(8,128)(2,1)S(1)} copy-done((bf16[1,32,8,512]{3,2,1,0:T(8,128)(2,1)S(1)}, bf16[1,32,8,512]{3,2,1,0:T(8,128)(2,1)}, u32[]{:S(2)}) %copy-start.2) | copy-done | bytes 262168
  2.6 0.0 copy-start.3
  2.6 0.9 %copy-done.3 = bf16[1,32,8,512]{3,2,1,0:T(8,128)(2,1)S(1)} copy-done((bf16[1,32,8,512]{3,2,1,0:T(8,128)(2,1)S(1)}, bf16[1,32,8,512]{3,2,1,0:T(8,128)(2,1)}, u32[]{:S(2)}) %copy-start.3) | copy-done | bytes 262168
  3.5 22.0 %shard_map.109 = (bf16[14,4,8,512]{3,2,1,0:T(8,128)(2,1)S(1)}, bf16[8,4,8,512]{3,2,1,0:T(8,128)(2,1)S(1)}) custom-call(bf16[32,8,512]{2,1,0:T(8,128)(2,1)S(1)} %bitcast.9, bf16[32,8,512]{2,1,0:T(8,128)(2,1)S(1)} %bitcast.10), custom_call_target="tpu_custom_call" | custom-call | tf_op jit(solution)/shard_map/pallas_call | solution.py:661
  25.5 0.0 copy-start
  25.5 1.1 %copy-done = bf16[512,768]{1,0:T(8,128)(2,1)S(1)} copy-done((bf16[512,768]{1,0:T(8,128)(2,1)S(1)}, bf16[512,768]{1,0:T(8,128)(2,1)}, u32[]{:S(2)}) %copy-start) | copy-done | bytes 786456
  26.7 0.0 copy-start.1
  26.7 0.9 %copy-done.1 = bf16[256,512]{1,0:T(8,128)(2,1)S(1)} copy-done((bf16[256,512]{1,0:T(8,128)(2,1)S(1)}, bf16[256,512]{1,0:T(8,128)(2,1)}, u32[]{:S(2)}) %copy-start.1) | copy-done | bytes 262168
  27.6 0.0 copy-start.4
  27.6 0.7 copy-done.4
  28.3 7.4 %shard_map.110 = (bf16[8,4,8,512]{3,2,1,0:T(8,128)(2,1)S(1)}, f32[8,32,512]{2,1,0:T(8,128)S(1)}, bf16[8,4,8,512]{3,2,1,0:T(8,128)(2,1)S(1)}, f32[512,768]{1,0:T(...) custom-call(bf16[14,4,8,512]{3,2,1,0:T(8,128)(2,1)S(1)} %get-tuple-element.21.fp_ref, ...), custom_call_target="tpu_custom_call" | custom-call | tf_op jit(solution)/shard_map/pallas_call | solution.py:661
  35.7 9.6 %shard_map.111 = (bf16[3,4,8,512]{3,2,1,0:T(8,128)(2,1)S(1)}, bf16[3,4,8,512]{3,2,1,0:T(8,128)(2,1)S(1)}) custom-call(bf16[8,4,8,512]{3,2,1,0:T(8,128)(2,1)S(1)} %get-tuple-element.25.g_ref), custom_call_target="tpu_custom_call" | custom-call | tf_op jit(solution)/shard_map/pallas_call | solution.py:661
  45.3 5.2 %shard_map.112 = (bf16[8,4,8,512]{3,2,1,0:T(8,128)(2,1)S(1)}, bf16[16,32,1152]{2,1,0:T(8,128)(2,1)S(1)}) custom-call(bf16[14,4,8,512]{3,2,1,0:T(8,128)(2,1)S(1)} %get-tuple-element.21.fp_ref, f32[8,32,512]{2,1,0:T(8,128)S(1)} %get-tuple-element.24.gu_ref, bf16[3,4,8,512]{3,2,1,0:T(8,128)(2,1)S(1)} %get-tuple-element.26.top_ref, ...), custom_call_target="tpu_custom_call" | custom-call | tf_op jit(solution)/shard_map/pallas_call | solution.py:661
  50.5 37.1 %shard_map.113 = (bf16[32,8,512]{2,1,0:T(8,128)(2,1)S(1)}, bf16[32,8,512]{2,1,0:T(8,128)(2,1)S(1)}, bf16[16,32,1152]{2,1,0:T(8,128)(2,1)S(1)}) custom-call(bf16[8,4,8,512]{3,2,1,0:T(8,128)(2,1)S(1)} %get-tuple-element.23.result_ref, bf16[8,4,8,512]{3,2,1,0:T(8,128)(2,1)S(1)} %get-tuple-element.31.gf_ref, bf16[16,32,1152]{2,1,0:T(8,128)(2,1)S(1)} %get-tuple-element.32.big), custom_call_target="tpu_custom_call" | custom-call | tf_op jit(solution)/shard_map/pallas_call | solution.py:661
  87.6 0.3 bitcast_convert_fusion
  87.8 0.6 pad_maximum_fusion.2
  88.5 0.7 reshape.26
  89.2 1.3 %slice.36 = f32[512,768]{1,0:T(8,128)} slice(f32[512,1152]{1,0:T(8,128)S(1)} %bitcast_convert_fusion), slice={[0:512], [0:768]} | slice | bytes 3145728 | tf_op jit(solution)/shard_map/slice | solution.py:523
  90.4 0.9 pad_maximum_fusion
  91.3 0.7 copy.14
  92.0 0.7 copy.15
  (4 shorter events, 0.1 us)
Async XLA Ops:
  1.6 1.0 %copy-start.2 = (bf16[1,32,8,512]{3,2,1,0:T(8,128)(2,1)S(1)}, bf16[1,32,8,512]{3,2,1,0:T(8,128)(2,1)}, u32[]{:S(2)}) copy-start(bf16[1,32,8,512]{3,2,1,0:T(8,128)(2,1)} %param.6) | copy-start | bytes 786436
  2.6 0.9 %copy-start.3 = (bf16[1,32,8,512]{3,2,1,0:T(8,128)(2,1)S(1)}, bf16[1,32,8,512]{3,2,1,0:T(8,128)(2,1)}, u32[]{:S(2)}) copy-start(bf16[1,32,8,512]{3,2,1,0:T(8,128)(2,1)} %param.7) | copy-start | bytes 786436
  25.5 1.1 %copy-start = (bf16[512,768]{1,0:T(8,128)(2,1)S(1)}, bf16[512,768]{1,0:T(8,128)(2,1)}, u32[]{:S(2)}) copy-start(bf16[512,768]{1,0:T(8,128)(2,1)} %wq_ref.1) | copy-start | bytes 2359300
  26.7 0.9 %copy-start.1 = (bf16[256,512]{1,0:T(8,128)(2,1)S(1)}, bf16[256,512]{1,0:T(8,128)(2,1)}, u32[]{:S(2)}) copy-start(bf16[256,512]{1,0:T(8,128)(2,1)} %wo_ref.1) | copy-start | bytes 786436
  27.6 0.7 copy-start.4

commit v2 on v0

--- a/solution.py
+++ b/solution.py
@@ -1,6 +1,11 @@
+import functools
+import itertools
+
 import jax
 import jax.numpy as jnp
 from jax import lax
+from jax.experimental import pallas as pl
+from jax.experimental.pallas import tpu as pltpu
 from jax.sharding import PartitionSpec as P
 
 HEADS = 4
@@ -112,7 +117,7 @@
     )
 
 
-def on_device(fields, cotangent, conv_weight, norm_gain, w_qkv, w_out):
+def on_device_native(fields, cotangent, conv_weight, norm_gain, w_qkv, w_out):
     batch_count, lat_rows, lon_cols, channels = fields.shape
     att_width = w_out.shape[0]
     wide = with_halo(fields, (("lon", 2),), 3, True)
@@ -174,6 +179,604 @@
     return (result, grad_fields, totals[0], totals[1], totals[2], totals[3])
 
 
+MESH = pl.DeviceIdType.MESH
+AXES = ("lat", "lon", "dp")
+LANES = 128
+
+
+def place():
+    return tuple(lax.axis_index(a) for a in AXES)
+
+
+def greet(sizes):
+    me = place()
+    barrier = pltpu.get_barrier_semaphore()
+    count = 0
+    for offset in itertools.product(*(range(s) for s in sizes)):
+        if not any(offset):
+            continue
+        target = {a: lax.rem(m + o, s) for a, m, o, s in zip(AXES, me, offset, sizes)}
+        pl.semaphore_signal(barrier, inc=1, device_id=target, device_id_type=MESH)
+        count += 1
+    pl.semaphore_wait(barrier, count)
+
+
+def remote(src, dst, send, recv, target):
+    return pltpu.make_async_remote_copy(
+        src_ref=src, dst_ref=dst, send_sem=send, recv_sem=recv, device_id=target, device_id_type=MESH
+    )
+
+
+def bring_rows(sizes, f_ref, c_ref, fp_ref, cr_ref, send, recv, xsend, xrecv, local):
+    n_lat, n_lon, _ = sizes
+    lat, lon, _ = place()
+    rows = f_ref.shape[0]
+    own = rows // n_lon
+
+    def span(j):
+        low, high = max(0, own * j - 3), min(rows, own * j + own + 3)
+        start = low - (own * j - 3)
+        return slice(low, high), slice(start, start + high - low)
+
+    def fields_copy(i, j):
+        there, here = span(j)
+        return remote(f_ref.at[there], fp_ref.at[here, i], send.at[0, j], recv.at[0, i], {"lon": j})
+
+    def cot_copy(i, j):
+        return remote(
+            c_ref.at[own * j : own * j + own], cr_ref.at[:, i], send.at[1, j], recv.at[1, i], {"lon": j}
+        )
+
+    def fields_own(j):
+        there, here = span(j)
+        return pltpu.make_async_copy(f_ref.at[there], fp_ref.at[here, j], local.at[0])
+
+    def cot_own(j):
+        return pltpu.make_async_copy(c_ref.at[own * j : own * j + own], cr_ref.at[:, j], local.at[1])
+
+    def below(i):
+        return remote(
+            f_ref.at[rows - 3 : rows], fp_ref.at[0:3, i], xsend.at[0], xrecv.at[0, i],
+            {"lat": lat + 1, "lon": 0},
+        )
+
+    def above(i):
+        return remote(
+            f_ref.at[0:3], fp_ref.at[own + 3 : own + 6, i], xsend.at[1], xrecv.at[1, i],
+            {"lat": lat - 1, "lon": n_lon - 1},
+        )
+
+    def start():
+        for j in range(n_lon):
+
+            @pl.when(lon != j)
+            def _(j=j):
+                fields_copy(lon, j).start()
+
+        @pl.when(lat < n_lat - 1)
+        def _():
+            below(lon).start()
+
+        @pl.when(lat > 0)
+        def _():
+            above(lon).start()
+
+        for j in range(n_lon):
+
+            @pl.when(lon != j)
+            def _(j=j):
+                cot_copy(lon, j).start()
+
+            @pl.when(lon == j)
+            def _(j=j):
+                fields_own(j).start()
+                cot_own(j).start()
+
+        @pl.when((lat == 0) & (lon == 0))
+        def _():
+            fp_ref[0:3] = jnp.zeros((3,) + fp_ref.shape[1:], fp_ref.dtype)
+
+        @pl.when((lat == n_lat - 1) & (lon == n_lon - 1))
+        def _():
+            fp_ref[own + 3 : own + 6] = jnp.zeros((3,) + fp_ref.shape[1:], fp_ref.dtype)
+
+    def wait_fields():
+        for j in range(n_lon):
+
+            @pl.when(lon == j)
+            def _(j=j):
+                fields_own(j).wait()
+                for i in range(n_lon):
+                    if i != j:
+                        fields_copy(i, j).wait_recv()
+
+        @pl.when((lat > 0) & (lon == 0))
+        def _():
+            for i in range(n_lon):
+                below(i).wait_recv()
+
+        @pl.when((lat < n_lat - 1) & (lon == n_lon - 1))
+        def _():
+            for i in range(n_lon):
+                above(i).wait_recv()
+
+    def wait_cot():
+        for j in range(n_lon):
+
+            @pl.when(lon == j)
+            def _(j=j):
+                cot_own(j).wait()
+                for i in range(n_lon):
+                    if i != j:
+                        cot_copy(i, j).wait_recv()
+
+    def wait_sent():
+        for j in range(n_lon):
+
+            @pl.when(lon != j)
+            def _(j=j):
+                fields_copy(lon, j).wait_send()
+                cot_copy(lon, j).wait_send()
+
+        @pl.when(lat < n_lat - 1)
+        def _():
+            below(lon).wait_send()
+
+        @pl.when(lat > 0)
+        def _():
+            above(lon).wait_send()
+
+    return start, wait_fields, wait_cot, wait_sent
+
+
+def convolve(pad, weight, out, own, flip):
+    circle, channels = pad.shape[1], pad.shape[2]
+    for c in range(channels // LANES):
+        lanes = slice(c * LANES, (c + 1) * LANES)
+
+        def row(r, carry, lanes=lanes):
+            bands = [pad[r + a, :, lanes] for a in range(7)]
+            total = bands[3]
+            for e in range(7):
+                part = None
+                for a in range(7):
+                    tap = weight[6 - a if flip else a, (6 - e if flip else e) : (7 - e if flip else e + 1), lanes]
+                    term = bands[a] * tap
+                    part = term if part is None else part + term
+                turn = (3 - e) % circle
+                if turn:
+                    part = pltpu.roll(part, turn, 0)
+                total = total + part
+            out[r, :, lanes] = total
+            return carry
+
+        lax.fori_loop(0, own, row, 0)
+
+
+def correlate_rows(pad, upstream, out, own):
+    circle, channels = pad.shape[1], pad.shape[2]
+
+    def chunk(c, carry):
+        lanes = pl.ds(pl.multiple_of(c * LANES, LANES), LANES)
+        for e in range(7):
+            turn = (e - 3) % circle
+            turned = [upstream[r, :, lanes] for r in range(own)]
+            if turn:
+                turned = [pltpu.roll(t, turn, 0) for t in turned]
+            for a in range(7):
+                total = None
+                for r in range(own):
+                    term = pad[r + a, :, lanes] * turned[r]
+                    total = term if total is None else total + term
+                out[a, e : e + 1, lanes] = jnp.sum(total, axis=0, keepdims=True)
+        return carry
+
+    lax.fori_loop(0, channels // LANES, chunk, 0)
+
+
+def dot(left, right, dims):
+    return lax.dot_general(left, right, (dims, ((), ())), preferred_element_type=jnp.float32)
+
+
+PLAIN, COLS, ROWS = ((1,), (0,)), ((1,), (1,)), ((0,), (0,))
+
+
+def attend_rows(projected, grad_mixed, circle, att_width):
+    cells = projected.shape[0]
+    group = max(circle, LANES)
+    row_of = lax.broadcasted_iota(jnp.int32, (group, group), 0) // circle
+    col_of = lax.broadcasted_iota(jnp.int32, (group, group), 1) // circle
+    same = row_of == col_of
+    lane_head = lax.broadcasted_iota(jnp.int32, (group, LANES), 1) // HEAD_DIM
+    bf16 = jnp.bfloat16
+    mixed, grads = [], []
+    for g in range(cells // group):
+        cut = slice(g * group, (g + 1) * group)
+        mixed_row, grad_q, grad_k, grad_v = [], [], [], []
+        for pair in range(att_width // LANES):
+            at = slice(pair * LANES, (pair + 1) * LANES)
+            q = projected[cut, :att_width][:, at]
+            k = projected[cut, att_width : 2 * att_width][:, at]
+            v = projected[cut, 2 * att_width :][:, at]
+            up = grad_mixed[cut, at]
+            parts = [[], [], [], []]
+            for h in range(LANES // HEAD_DIM):
+                mine = lane_head == h
+                zero = jnp.zeros((), bf16)
+                scores = dot(jnp.where(mine, q, zero), k, COLS) * HEAD_DIM ** (-0.5)
+                scores = jnp.where(same, scores, -jnp.inf)
+                raised = jnp.exp(scores - jnp.max(scores, -1, keepdims=True))
+                probs = raised / jnp.sum(raised, -1, keepdims=True)
+                weights = probs.astype(bf16)
+                grad_probs = dot(jnp.where(mine, up, zero), v, COLS)
+                inner = jnp.sum(probs * grad_probs, -1, keepdims=True)
+                grad_scores = (probs * (grad_probs - inner) * HEAD_DIM ** (-0.5)).astype(bf16)
+                parts[0].append(dot(weights, v, PLAIN))
+                parts[1].append(dot(grad_scores, k, PLAIN))
+                parts[2].append(dot(grad_scores, q, ROWS))
+                parts[3].append(dot(weights, up, ROWS))
+            for part, found in zip(parts, (mixed_row, grad_q, grad_k, grad_v)):
+                whole = part[0]
+                for h in range(1, len(part)):
+                    whole = jnp.where(lane_head == h, part[h], whole)
+                found.append(whole.astype(bf16))
+        mixed.append(jnp.concatenate(mixed_row, axis=1))
+        grads.append(jnp.concatenate(grad_q + grad_k + grad_v, axis=1))
+    return jnp.concatenate(mixed, axis=0), jnp.concatenate(grads, axis=0)
+
+
+def core_step(cr_ref, update_ref, gain, wq_ref, wo_ref, result_ref, gu_ref, gub_ref, gq_ref, go_ref, gg_ref):
+    own, blocks, width, channels = cr_ref.shape
+    circle, cells = blocks * width, own * blocks * width
+    att_width = wo_ref.shape[0]
+    update = update_ref[...].reshape(cells, channels)
+    inverse = lax.rsqrt(jnp.mean(update * update, -1, keepdims=True) + EPSILON)
+    normed = (update * inverse * gain).astype(jnp.bfloat16)
+    projected = dot(normed, wq_ref[...], PLAIN).astype(jnp.bfloat16)
+    yield
+    cot32 = cr_ref[...].astype(jnp.float32).reshape(cells, channels)
+    cot = cot32.astype(jnp.bfloat16)
+    grad_mixed = dot(cot, wo_ref[...], COLS).astype(jnp.bfloat16)
+    mixed, grad_projected = attend_rows(projected, grad_mixed, circle, att_width)
+    grad_normed = dot(grad_projected, wq_ref[...], COLS)
+    gained = gain * grad_normed
+    grad_update = (
+        cot32
+        + inverse * gained
+        - update * (inverse * inverse * inverse) * jnp.mean(gained * update, -1, keepdims=True)
+    )
+    gu_ref[...] = grad_update.reshape(gu_ref.shape)
+    gub_ref[...] = grad_update.reshape(gub_ref.shape).astype(jnp.bfloat16)
+    yield
+    result = update + dot(mixed, wo_ref[...], PLAIN)
+    result_ref[...] = result.reshape(result_ref.shape).astype(jnp.bfloat16)
+    yield
+    gg_ref[...] = jnp.sum(grad_normed * (update * inverse), axis=0, keepdims=True)
+    go_ref[...] = dot(mixed, cot, ROWS)
+    gq_ref[...] = dot(normed, grad_projected, ROWS)
+    yield
+
+
+def halo_rows(sizes, g_ref, top_ref, low_ref, send, recv):
+    n_lat, n_lon, _ = sizes
+    lat, lon, _ = place()
+    own = g_ref.shape[0]
+    index, last = lat * n_lon + lon, n_lat * n_lon - 1
+
+    def at(k):
+        k = lax.rem(k + n_lat * n_lon, n_lat * n_lon)
+        return {"lat": k // n_lon, "lon": lax.rem(k, n_lon)}
+
+    down = remote(g_ref.at[own - 3 : own], top_ref, send.at[0], recv.at[0], at(index + 1))
+    up = remote(g_ref.at[0:3], low_ref, send.at[1], recv.at[1], at(index - 1))
+
+    def start():
+        @pl.when(index < last)
+        def _():
+            down.start()
+
+        @pl.when(index > 0)
+        def _():
+            up.start()
+
+        @pl.when(index == 0)
+        def _():
+            top_ref[...] = jnp.zeros_like(top_ref)
+
+        @pl.when(index == last)
+        def _():
+            low_ref[...] = jnp.zeros_like(low_ref)
+
+    def wait():
+        @pl.when(index > 0)
+        def _():
+            down.wait_recv()
+            up.wait_send()
+
+        @pl.when(index < last)
+        def _():
+            up.wait_recv()
+            down.wait_send()
+
+    return start, wait
+
+
+def pack(bigs, gq_ref, go_ref, conv, gg_ref):
+    parts, rows, first = bigs[0].shape
+    whole = parts * rows
+    wide = gq_ref.shape[1]
+    att, channels = go_ref.shape
+    bf16 = jnp.bfloat16
+    fold = whole // att
+    part = channels // fold
+    rest = wide - first
+    bigs[0][...] = gq_ref[:, :first].reshape(parts, rows, first).astype(bf16)
+    bigs[1][:, :, :rest] = gq_ref[:, first:].reshape(parts, rows, rest).astype(bf16)
+    for k in range(fold):
+        piece = go_ref[:, k * part : (k + 1) * part].astype(bf16).reshape(parts // fold, rows, part)
+        bigs[1][k * (parts // fold) : (k + 1) * (parts // fold), :, rest : rest + part] = piece
+    small = jnp.concatenate(
+        [conv[a] for a in range(7)] + [gg_ref[...], jnp.zeros((64 - 50, channels), jnp.float32)], axis=0
+    )
+    step = 64 // rows
+    bigs[1][:, :, rest + part :] = jnp.zeros((parts, rows, LANES), bf16)
+    for k in range(channels // LANES):
+        piece = small[:, k * LANES : (k + 1) * LANES].astype(bf16).reshape(step, rows, LANES)
+        bigs[1][k * step : (k + 1) * step, :, rest + part :] = piece
+
+
+def finish(one_ref, two_ref, result_ref, gf_ref, result_out, gf_out, gq_out, go_out, gc_out, gg_out):
+    parts, rows, first = one_ref.shape
+    whole = parts * rows
+    wide = gq_out.shape[1]
+    att, channels = go_out.shape
+    fold = whole // att
+    part = channels // fold
+    rest = wide - first
+    f32 = jnp.float32
+    result_out[...] = result_ref[...]
+    gf_out[...] = gf_ref[...]
+    gq_out[:, :first] = one_ref[...].astype(f32).reshape(whole, first)
+    gq_out[:, first:] = two_ref[:, :, :rest].astype(f32).reshape(whole, rest)
+    for k in range(fold):
+        piece = two_ref[k * (parts // fold) : (k + 1) * (parts // fold), :, rest : rest + part]
+        go_out[:, k * part : (k + 1) * part] = piece.astype(f32).reshape(att, part)
+    step = 64 // rows
+    for k in range(channels // LANES):
+        lanes = slice(k * LANES, (k + 1) * LANES)
+        small = two_ref[k * step : (k + 1) * step, :, rest + part :].astype(f32).reshape(64, LANES)
+        for a in range(7):
+            gc_out[a, :, lanes] = small[a * 7 : (a + 1) * 7]
+        gg_out[:, lanes] = small[49:50]
+
+
+def halving(turns, big, every, got, held, send, recv):
+    f32 = jnp.float32
+    count = len(turns)
+    sizes = [big.shape[0] >> (k + 1) for k in range(count)]
+    base = [0]
+    for n in sizes[:-1]:
+        base.append(base[-1] + n)
+    starts = [jnp.int32(0)]
+    for (_, bit), n in zip(turns, sizes):
+        starts.append(starts[-1] + bit * n)
+
+    def source(k, at, n):
+        return big.at[pl.ds(at, n)] if k == 0 else held.at[pl.ds(base[k - 1] + at, n)]
+
+    def down(k):
+        target, bit = turns[k]
+        n = sizes[k]
+        return remote(
+            source(k, (1 - bit) * n, n), got.at[base[k] : base[k] + n], send.at[k], recv.at[k], target
+        )
+
+    def back(k, mine):
+        target, bit = turns[k]
+        n = sizes[k]
+        spot = every.at[pl.ds(starts[k] + (bit if mine else 1 - bit) * n, n)]
+        return remote(spot, spot, send.at[count + k], recv.at[count + k], target)
+
+    def add(k):
+        bit, n = turns[k][1], sizes[k]
+        down(k).wait()
+        for i in range(n):
+            at = bit * n + i
+            mine = big[at] if k == 0 else held[base[k - 1] + at]
+            total = (mine.astype(f32) + got[base[k] + i].astype(f32)).astype(big.dtype)
+            if k == count - 1:
+                every[starts[count] + i] = total
+            else:
+                held[base[k] + i] = total
+        if k == count - 1:
+            back(k, True).start()
+        else:
+            down(k + 1).start()
+
+    def gather(k):
+        back(k, True).wait_send()
+        back(k, False).wait_recv()
+        if k:
+            back(k - 1, True).start()
+
+    stages = [lambda: down(0).start()]
+    stages += [functools.partial(add, k) for k in range(count)]
+    stages += [functools.partial(gather, k) for k in reversed(range(count))]
+    return stages
+
+
+def give_rows(n_lon, lon, src, dst, send, recv):
+    own = src.shape[0]
+
+    def copy(i, j):
+        return remote(src.at[:, j], dst.at[pl.ds(i * own, own)], send.at[j], recv.at[i], {"lon": j})
+
+    def start():
+        for j in range(n_lon):
+
+            @pl.when(lon != j)
+            def _(j=j):
+                copy(lon, j).start()
+
+            @pl.when(lon == j)
+            def _(j=j):
+                dst[j * own : (j + 1) * own] = src[:, j]
+
+    def wait():
+        for j in range(n_lon):
+
+            @pl.when(lon == j)
+            def _(j=j):
+                for i in range(n_lon):
+                    if i != j:
+                        copy(i, j).wait_recv()
+
+            @pl.when(lon != j)
+            def _(j=j):
+                copy(lon, j).wait_send()
+
+    return start, wait
+
+
+def layer(sizes, f_ref, c_ref, w_hbm, gain_ref, wq_hbm, wo_hbm,
+          result_out, gf_out, every1, every2,
+          fp, cr, weight, wq, wo, pad, update, result, gu, gub, gq, go, gg, top, low, gpad, out, gf, conv,
+          big1, got1, held1, big2, got2, held2,
+          send, recv, xsend, xrecv, local, hsend, hrecv, rsend, rrecv, gsend, grecv, s1, r1, s2, r2):
+    n_lat, n_lon, _ = sizes
+    lat, lon, dp = place()
+    own, circle, channels = gu.shape
+    f32, bf16 = jnp.float32, jnp.bfloat16
+    loads = [
+        pltpu.make_async_copy(src, dst, local.at[2 + k])
+        for k, (src, dst) in enumerate(((w_hbm, weight), (wq_hbm, wq), (wo_hbm, wo)))
+    ]
+    for load in loads:
+        load.start()
+    odd, high = lax.rem(lon, 2), lon // 2
+    by_dp = ({"dp": 1 - dp}, dp)
+    by_lat = ({"lat": 1 - lat}, lat)
+    by_odd = ({"lon": lon + 1 - 2 * odd}, odd)
+    by_high = ({"lon": lon + 2 - 4 * high}, high)
+    one = halving((by_dp, by_lat, by_odd, by_high), big1, every1, got1, held1, s1, r1)
+    two = halving((by_dp, by_odd, by_high, by_lat), big2, every2, got2, held2, s2, r2)
+    start_in, wait_fields, wait_cot, wait_sent = bring_rows(
+        sizes, f_ref, c_ref, fp, cr, send, recv, xsend, xrecv, local
+    )
+    start_h, wait_h = halo_rows(sizes, gub, top, low, hsend, hrecv)
+    start_r, wait_r = give_rows(n_lon, lon, result, result_out, rsend, rrecv)
+    start_g, wait_g = give_rows(n_lon, lon, gf, gf_out, gsend, grecv)
+    greet(sizes)
+    start_in()
+    loads[0].wait()
+    wait_fields()
+    pad[...] = fp[...].astype(f32).reshape(pad.shape)
+    convolve(pad, weight, update, own, False)
+    for load in loads[1:]:
+        load.wait()
+    steps = core_step(cr, update, gain_ref[...], wq, wo, result, gu, gub, gq, go, gg)
+    next(steps)
+    wait_cot()
+    next(steps)
+    start_h()
+    next(steps)
+    start_r()
+    next(steps)
+    correlate_rows(pad, gu, conv, own)
+    pack((big1, big2), gq, go, conv, gg)
+    one[0]()
+    two[0]()
+    wait_h()
+    gpad[0:3] = top[...].astype(f32).reshape((3, circle, channels))
+    gpad[3 : own + 3] = gu[...]
+    gpad[own + 3 :] = low[...].astype(f32).reshape((3, circle, channels))
+    one[1]()
+    two[1]()
+    convolve(gpad, weight, out, own, True)
+    gf[...] = out[...].reshape(gf.shape).astype(bf16)
+    start_g()
+    for stage_one, stage_two in zip(one[2:], two[2:]):
+        stage_one()
+        stage_two()
+    wait_sent()
+    wait_r()
+    wait_g()
+
+
+def on_device(sizes, fields, cotangent, conv_weight, norm_gain, w_qkv, w_out):
+    n_lat, n_lon, n_dp = sizes
+    batch, rows, cols, channels = fields.shape
+    own, circle = rows // n_lon, cols * n_lon
+    att = w_out.shape[0]
+    bf16, f32 = jnp.bfloat16, jnp.float32
+    shape = jax.ShapeDtypeStruct
+    sems = pltpu.SemaphoreType.DMA
+    vmem = pltpu.VMEM
+    parts = n_lat * n_lon * n_dp
+    part_rows = channels // parts
+    wide = w_qkv.shape[1] + att * att // channels * (channels // att) + LANES
+    first = (wide // LANES + 1) // 2 * LANES
+    widths = (first, wide - first)
+    turns = 2 + 2
+    blocked = (own, n_lon, cols, channels)
+    flat = (own, circle, channels)
+    padded = (own + 6, circle, channels)
+    sums = []
+    for w in widths:
+        sums += [vmem((n, part_rows, w), bf16) for n in (parts, parts, parts)]
+    inside = pl.BlockSpec(memory_space=pltpu.VMEM)
+    outside = pl.BlockSpec(memory_space=pl.ANY)
+    result, grad_fields, one, two = pl.pallas_call(
+        functools.partial(layer, sizes),
+        out_shape=[shape((rows, cols, channels), bf16)] * 2
+        + [shape((parts, part_rows, w), bf16) for w in widths],
+        in_specs=[outside, outside, outside, inside, outside, outside],
+        out_specs=[inside] * 4,
+        scratch_shapes=[
+            vmem((own + 6,) + blocked[1:], bf16), vmem(blocked, bf16), vmem(conv_weight.shape, f32),
+            vmem(w_qkv.shape, bf16), vmem(w_out.shape, bf16),
+            vmem(padded, f32), vmem(flat, f32), vmem(blocked, bf16), vmem(flat, f32), vmem(blocked, bf16),
+            vmem(w_qkv.shape, f32), vmem(w_out.shape, f32), vmem((1, channels), f32),
+            vmem((3,) + blocked[1:], bf16), vmem((3,) + blocked[1:], bf16),
+            vmem(padded, f32), vmem(flat, f32), vmem(blocked, bf16), vmem(conv_weight.shape, f32),
+        ] + sums + [
+            sems((2, n_lon)), sems((2, n_lon)), sems((2,)), sems((2, n_lon)), sems((5,)),
+            sems((2,)), sems((2,)),
+            sems((n_lon,)), sems((n_lon,)), sems((n_lon,)), sems((n_lon,)),
+            sems((2 * turns,)), sems((2 * turns,)), sems((2 * turns,)), sems((2 * turns,)),
+        ],
+        compiler_params=pltpu.CompilerParams(
+            vmem_limit_bytes=48 * 2**20, collective_id=1, has_side_effects=True
+        ),
+    )(fields[0], cotangent[0], conv_weight, norm_gain.reshape(1, channels), w_qkv, w_out)
+    outs = pl.pallas_call(
+        finish,
+        out_shape=[shape((rows, cols, channels), bf16)] * 2
+        + [shape(w_qkv.shape, f32), shape(w_out.shape, f32), shape(conv_weight.shape, f32),
+           shape((1, channels), f32)],
+        in_specs=[inside] * 4,
+        out_specs=[inside] * 6,
+        compiler_params=pltpu.CompilerParams(vmem_limit_bytes=32 * 2**20),
+    )(one, two, result, grad_fields)
+    return outs[0][None], outs[1][None], outs[2], outs[3], outs[4], outs[5].reshape(channels)
+
+
+def pick(mesh, *args):
+    sizes = tuple(mesh.shape[a] for a in AXES)
+    _, rows, cols, channels = args[0].shape
+    att = args[5].shape[0]
+    n_lat, n_lon, n_dp = sizes
+    parts = n_lat * n_lon * n_dp
+    fits = (
+        args[0].shape[0] == 1 and n_lat == 2 and n_dp == 2 and n_lon == 4
+        and rows % n_lon == 0 and rows // n_lon >= 3 and cols % 8 == 0
+        and LANES % (cols * n_lon) == 0 and (rows // n_lon * cols * n_lon) % LANES == 0
+        and channels == 2 * att and channels % (8 * parts) == 0 and 64 % (channels // parts) == 0
+        and att % LANES == 0
+    )
+    return on_device(sizes, *args) if fits else on_device_native(*args)
+
+
 def solution(mesh):
     placed = (
         P(("member", "dp"), "lat", "lon", None),
@@ -184,7 +787,7 @@
         P(),
     )
     return jax.shard_map(
-        on_device,
+        functools.partial(pick, mesh),
         mesh=mesh,
         in_specs=placed,
         out_specs=(

time: 234 us -> 73.5 us (0.31)
  waiting for transfers between devices: 80.2 us -> 0 us
  Pallas kernels: 0 us -> 67 us
  starting transfers between devices: 35 us -> 0 us
  blocking collectives: 31.5 us -> 0 us
  other arithmetic: 25.8 us -> 0 us
  local copies, waits for them, and re-layouts: 25.9 us -> 5.55 us
  matrix products: 19.2 us -> 0 us
  between operations: 15.5 us -> 0.66 us
    pallas_call x0 -> x2, Pallas kernels: none -> 67 us  [the longest x1 65.4 us: on_device(): pl.pallas_call(functools.partial(layer, sizes), out_shape=[shape((rows, c...]
    psum x1 -> x0, waiting for transfers between devices: 64.3 us -> none  [on_device(): lax.psum((grad_weight, grad_out, grad_conv, grad_gain), ('lon', 'lat', 'd...]
    psum x1 -> x0, blocking collectives: 31.5 us -> none  [on_device(): lax.psum((grad_weight, grad_out, grad_conv, grad_gain), ('lon', 'lat', 'd...]
    all_to_all x4 -> x0, starting transfers between devices: 17.9 us -> none  [the longest x1 5.04 us: on_device(): lax.all_to_all(grad_projected_rows, 'lon', split_axis=2, concat_axis=1, t...]
    ppermute x8 -> x0, starting transfers between devices: 17.1 us -> none  [the longest x4 9.14 us: with_halo(): before = lax.ppermute(last, axis, up)]
    dot_general x11 -> x0, matrix products: 17.1 us -> none  [the longest x2 2.97 us: contract_cols(): lax.dot_general(left, right, (((1,), (1,)), ((), ())), preferred_element_...]
    reduce_sum x4 -> x0, other arithmetic: 16.4 us -> none  [the longest x1 10.5 us: on_device(): inverse = lax.rsqrt(jnp.mean(update * update, -1, keepdims=True) + EPSILON)]
    all_to_all x4 -> x0, waiting for transfers between devices: 10.4 us -> none  [the longest x1 6.17 us: on_device(): lax.all_to_all(projected.reshape(batch_count, lat_rows, lon_cols, 3 * att...]
  transfers between devices with their start and end apart: 13 -> 0, of which waited for: 6 -> 0; matrix products, arithmetic and copies ran while one was open for 19% -> 0% of each run, Pallas kernels for 0% -> 0%
where the time goes in v2:
time: 73.5 us; the launch traced here: 73.2 us
  Pallas kernels  67 us (91%)
  local copies, waits for them, and re-layouts  5.55 us (8%)
    pallas_call x1, Pallas kernels, on_device(): pl.pallas_call(functools.partial(layer, sizes), out_shape=[shape((rows, c...  65.4 us
    unnamed x12, local copies, waits for them, and re-layouts  5.55 us
    pallas_call x1, Pallas kernels, on_device(): pl.pallas_call(finish, out_shape=[shape((rows, cols, channels), bf16)] *...  1.65 us

profile of v2, /device:TPU:0, one launch (start us, length us, event | category | flops | bytes accessed | tf_op | source)
XLA Modules:
  0.0 73.2 jit_solution(6667428181857279799)
XLA Ops:
  0.6 0.0 copy-start
  0.6 1.1 %copy-done = bf16[512,768]{1,0:T(8,128)(2,1)S(1)} copy-done((bf16[512,768]{1,0:T(8,128)(2,1)S(1)}, bf16[512,768]{1,0:T(8,128)(2,1)}, u32[]{:S(2)}) %copy-start) | copy-done | bytes 786456
  1.8 0.0 copy-start.1
  1.8 0.9 %copy-done.1 = bf16[1,32,8,512]{3,2,1,0:T(8,128)(2,1)S(1)} copy-done((bf16[1,32,8,512]{3,2,1,0:T(8,128)(2,1)S(1)}, bf16[1,32,8,512]{3,2,1,0:T(8,128)(2,1)}, u32[]{:S(2)}) %copy-start.1) | copy-done | bytes 262168
  2.7 0.0 copy-start.2
  2.7 0.9 %copy-done.2 = bf16[1,32,8,512]{3,2,1,0:T(8,128)(2,1)S(1)} copy-done((bf16[1,32,8,512]{3,2,1,0:T(8,128)(2,1)S(1)}, bf16[1,32,8,512]{3,2,1,0:T(8,128)(2,1)}, u32[]{:S(2)}) %copy-start.2) | copy-done | bytes 262168
  3.7 0.0 copy-start.3
  3.7 0.9 %copy-done.3 = bf16[256,512]{1,0:T(8,128)(2,1)S(1)} copy-done((bf16[256,512]{1,0:T(8,128)(2,1)S(1)}, bf16[256,512]{1,0:T(8,128)(2,1)}, u32[]{:S(2)}) %copy-start.3) | copy-done | bytes 262168
  4.6 0.0 copy-start.4
  4.6 0.9 %copy-done.4 = f32[7,7,512]{2,1,0:T(8,128)S(1)} copy-done((f32[7,7,512]{2,1,0:T(8,128)S(1)}, f32[7,7,512]{2,1,0:T(8,128)}, u32[]{:S(2)}) %copy-start.4) | copy-done | bytes 100376
  5.5 0.0 copy-start.5
  5.5 0.7 copy-done.5
  6.2 65.4 %shard_map.109 = (bf16[32,8,512]{2,1,0:T(8,128)(2,1)S(1)}, bf16[32,8,512]{2,1,0:T(8,128)(2,1)S(1)}, bf16[16,32,640]{2,1,0:T(8,128)(2,1)S(1)}, bf16[16,32,512]{2,1,0:T(8,128)(2,1)S(1)}) custom-call(bf16[32,8,512]{2,1,0:T(8,128)(2,1)S(1)} %bitcast.6, bf16[32,8,512]{2,1,0:T(8,128)(2,1)S(1)} %bitcast.7, f32[7,7,512]{2,1,0:T(8,128)S(1)} %copy-done.4, ...), custom_call_target="tpu_custom_call" | custom-call | tf_op jit(solution)/shard_map/pallas_call | solution.py:729
  71.6 1.7 %shard_map.110 = (bf16[32,8,512]{2,1,0:T(8,128)(2,1)}, bf16[32,8,512]{2,1,0:T(8,128)(2,1)}, f32[512,768]{1,0:T(8,128)}, f32[256,512]{1,0:T(8,128)}, f32[7,7,512]{2,1,0:T(8,128)}, /*index=5*/f32[1,512]{1,0:T(1,128)}) custom-call(bf16[16,32,640]{2,1,0:T(8,128)(2,1)S(1)} %get-tuple-element.16.one_ref, bf16[16,32,512]{2,1,0:T(8,128)(2,1)S(1)} %get-tuple-element.17.two_ref, ...), custom_call_target="tpu_custom_call" | custom-call | tf_op jit(solution)/shard_map/pallas_call | solution.py:752
Async XLA Ops:
  0.6 1.1 %copy-start = (bf16[512,768]{1,0:T(8,128)(2,1)S(1)}, bf16[512,768]{1,0:T(8,128)(2,1)}, u32[]{:S(2)}) copy-start(bf16[512,768]{1,0:T(8,128)(2,1)} %wq_hbm.1) | copy-start | bytes 2359300
  1.8 0.9 %copy-start.1 = (bf16[1,32,8,512]{3,2,1,0:T(8,128)(2,1)S(1)}, bf16[1,32,8,512]{3,2,1,0:T(8,128)(2,1)}, u32[]{:S(2)}) copy-start(bf16[1,32,8,512]{3,2,1,0:T(8,128)(2,1)} %param.6) | copy-start | bytes 786436
  2.7 0.9 %copy-start.2 = (bf16[1,32,8,512]{3,2,1,0:T(8,128)(2,1)S(1)}, bf16[1,32,8,512]{3,2,1,0:T(8,128)(2,1)}, u32[]{:S(2)}) copy-start(bf16[1,32,8,512]{3,2,1,0:T(8,128)(2,1)} %param.7) | copy-start | bytes 786436
  3.7 0.9 %copy-start.3 = (bf16[256,512]{1,0:T(8,128)(2,1)S(1)}, bf16[256,512]{1,0:T(8,128)(2,1)}, u32[]{:S(2)}) copy-start(bf16[256,512]{1,0:T(8,128)(2,1)} %wo_hbm.1) | copy-start | bytes 786436
  4.6 0.9 %copy-start.4 = (f32[7,7,512]{2,1,0:T(8,128)S(1)}, f32[7,7,512]{2,1,0:T(8,128)}, u32[]{:S(2)}) copy-start(f32[7,7,512]{2,1,0:T(8,128)} %w_hbm.1) | copy-start | bytes 301060
  5.5 0.7 copy-start.5

commit v3 on v2

--- a/solution.py
+++ b/solution.py
@@ -381,7 +381,7 @@
 PLAIN, COLS, ROWS = ((1,), (0,)), ((1,), (1,)), ((0,), (0,))
 
 
-def attend_rows(projected, grad_mixed, circle, att_width):
+def attend_rows(projected, circle, att_width):
     cells = projected.shape[0]
     group = max(circle, LANES)
     row_of = lax.broadcasted_iota(jnp.int32, (group, group), 0) // circle
@@ -389,43 +389,61 @@
     same = row_of == col_of
     lane_head = lax.broadcasted_iota(jnp.int32, (group, LANES), 1) // HEAD_DIM
     bf16 = jnp.bfloat16
-    mixed, grads = [], []
-    for g in range(cells // group):
-        cut = slice(g * group, (g + 1) * group)
-        mixed_row, grad_q, grad_k, grad_v = [], [], [], []
-        for pair in range(att_width // LANES):
-            at = slice(pair * LANES, (pair + 1) * LANES)
-            q = projected[cut, :att_width][:, at]
-            k = projected[cut, att_width : 2 * att_width][:, at]
-            v = projected[cut, 2 * att_width :][:, at]
-            up = grad_mixed[cut, at]
-            parts = [[], [], [], []]
-            for h in range(LANES // HEAD_DIM):
-                mine = lane_head == h
-                zero = jnp.zeros((), bf16)
-                scores = dot(jnp.where(mine, q, zero), k, COLS) * HEAD_DIM ** (-0.5)
+    zero = jnp.zeros((), bf16)
+    heads = range(LANES // HEAD_DIM)
+    groups = [slice(g * group, (g + 1) * group) for g in range(cells // group)]
+    pairs = [slice(p * LANES, (p + 1) * LANES) for p in range(att_width // LANES)]
+
+    def third(k, cut, at):
+        return projected[cut, k * att_width : (k + 1) * att_width][:, at]
+
+    def join(parts):
+        whole = parts[0]
+        for h in heads[1:]:
+            whole = jnp.where(lane_head == h, parts[h], whole)
+        return whole.astype(bf16)
+
+    kept, mixed = {}, []
+    for g, cut in enumerate(groups):
+        found = []
+        for p, at in enumerate(pairs):
+            q, k, v = (third(n, cut, at) for n in range(3))
+            parts = []
+            for h in heads:
+                scores = dot(jnp.where(lane_head == h, q, zero), k, COLS) * HEAD_DIM ** (-0.5)
                 scores = jnp.where(same, scores, -jnp.inf)
                 raised = jnp.exp(scores - jnp.max(scores, -1, keepdims=True))
                 probs = raised / jnp.sum(raised, -1, keepdims=True)
-                weights = probs.astype(bf16)
-                grad_probs = dot(jnp.where(mine, up, zero), v, COLS)
-                inner = jnp.sum(probs * grad_probs, -1, keepdims=True)
-                grad_scores = (probs * (grad_probs - inner) * HEAD_DIM ** (-0.5)).astype(bf16)
-                parts[0].append(dot(weights, v, PLAIN))
-                parts[1].append(dot(grad_scores, k, PLAIN))
-                parts[2].append(dot(grad_scores, q, ROWS))
-                parts[3].append(dot(weights, up, ROWS))
-            for part, found in zip(parts, (mixed_row, grad_q, grad_k, grad_v)):
-                whole = part[0]
-                for h in range(1, len(part)):
-                    whole = jnp.where(lane_head == h, part[h], whole)
-                found.append(whole.astype(bf16))
-        mixed.append(jnp.concatenate(mixed_row, axis=1))
-        grads.append(jnp.concatenate(grad_q + grad_k + grad_v, axis=1))
-    return jnp.concatenate(mixed, axis=0), jnp.concatenate(grads, axis=0)
-
-
-def core_step(cr_ref, update_ref, gain, wq_ref, wo_ref, result_ref, gu_ref, gub_ref, gq_ref, go_ref, gg_ref):
+                kept[g, p, h] = probs
+                parts.append(dot(probs.astype(bf16), v, PLAIN))
+            found.append(join(parts))
+        mixed.append(jnp.concatenate(found, axis=1))
+
+    def backward(grad_mixed):
+        grads = []
+        for g, cut in enumerate(groups):
+            found = [[], [], []]
+            for p, at in enumerate(pairs):
+                q, k, v = (third(n, cut, at) for n in range(3))
+                up = grad_mixed[cut, at]
+                parts = [[], [], []]
+                for h in heads:
+                    probs = kept[g, p, h]
+                    grad_probs = dot(jnp.where(lane_head == h, up, zero), v, COLS)
+                    inner = jnp.sum(probs * grad_probs, -1, keepdims=True)
+                    grad_scores = (probs * (grad_probs - inner) * HEAD_DIM ** (-0.5)).astype(bf16)
+                    parts[0].append(dot(grad_scores, k, PLAIN))
+                    parts[1].append(dot(grad_scores, q, ROWS))
+                    parts[2].append(dot(probs.astype(bf16), up, ROWS))
+                for part, into in zip(parts, found):
+                    into.append(join(part))
+            grads.append(jnp.concatenate(found[0] + found[1] + found[2], axis=1))
+        return jnp.concatenate(grads, axis=0)
+
+    return jnp.concatenate(mixed, axis=0), backward
+
+
+def core_step(cr_ref, update_ref, gain, wq_ref, wo_ref, result_ref, gu_ref, gub_ref, big1_ref, big3_ref, go_ref, gg_ref):
     own, blocks, width, channels = cr_ref.shape
     circle, cells = blocks * width, own * blocks * width
     att_width = wo_ref.shape[0]
@@ -433,11 +451,14 @@
     inverse = lax.rsqrt(jnp.mean(update * update, -1, keepdims=True) + EPSILON)
     normed = (update * inverse * gain).astype(jnp.bfloat16)
     projected = dot(normed, wq_ref[...], PLAIN).astype(jnp.bfloat16)
+    mixed, backward = attend_rows(projected, circle, att_width)
+    result = update + dot(mixed, wo_ref[...], PLAIN)
+    result_ref[...] = result.reshape(result_ref.shape).astype(jnp.bfloat16)
     yield
     cot32 = cr_ref[...].astype(jnp.float32).reshape(cells, channels)
     cot = cot32.astype(jnp.bfloat16)
     grad_mixed = dot(cot, wo_ref[...], COLS).astype(jnp.bfloat16)
-    mixed, grad_projected = attend_rows(projected, grad_mixed, circle, att_width)
+    grad_projected = backward(grad_mixed)
     grad_normed = dot(grad_projected, wq_ref[...], COLS)
     gained = gain * grad_normed
     grad_update = (
@@ -448,12 +469,13 @@
     gu_ref[...] = grad_update.reshape(gu_ref.shape)
     gub_ref[...] = grad_update.reshape(gub_ref.shape).astype(jnp.bfloat16)
     yield
-    result = update + dot(mixed, wo_ref[...], PLAIN)
-    result_ref[...] = result.reshape(result_ref.shape).astype(jnp.bfloat16)
+    grad_weight = dot(normed, grad_projected, ROWS).astype(jnp.bfloat16)
+    half = big1_ref.shape[2]
+    big1_ref[...] = grad_weight[:, :half].reshape(big1_ref.shape)
+    big3_ref[...] = grad_weight[:, half:].reshape(big3_ref.shape)
     yield
     gg_ref[...] = jnp.sum(grad_normed * (update * inverse), axis=0, keepdims=True)
     go_ref[...] = dot(mixed, cot, ROWS)
-    gq_ref[...] = dot(normed, grad_projected, ROWS)
     yield
 
 
@@ -501,110 +523,50 @@
     return start, wait
 
 
-def pack(bigs, gq_ref, go_ref, conv, gg_ref):
-    parts, rows, first = bigs[0].shape
-    whole = parts * rows
-    wide = gq_ref.shape[1]
+def pack(big, go_ref, conv, gg_ref):
+    parts, rows, _ = big.shape
     att, channels = go_ref.shape
     bf16 = jnp.bfloat16
-    fold = whole // att
+    fold = parts * rows // att
     part = channels // fold
-    rest = wide - first
-    bigs[0][...] = gq_ref[:, :first].reshape(parts, rows, first).astype(bf16)
-    bigs[1][:, :, :rest] = gq_ref[:, first:].reshape(parts, rows, rest).astype(bf16)
     for k in range(fold):
         piece = go_ref[:, k * part : (k + 1) * part].astype(bf16).reshape(parts // fold, rows, part)
-        bigs[1][k * (parts // fold) : (k + 1) * (parts // fold), :, rest : rest + part] = piece
+        big[k * (parts // fold) : (k + 1) * (parts // fold), :, :part] = piece
     small = jnp.concatenate(
         [conv[a] for a in range(7)] + [gg_ref[...], jnp.zeros((64 - 50, channels), jnp.float32)], axis=0
     )
     step = 64 // rows
-    bigs[1][:, :, rest + part :] = jnp.zeros((parts, rows, LANES), bf16)
+    used = channels // LANES * step
     for k in range(channels // LANES):
         piece = small[:, k * LANES : (k + 1) * LANES].astype(bf16).reshape(step, rows, LANES)
-        bigs[1][k * step : (k + 1) * step, :, rest + part :] = piece
-
-
-def finish(one_ref, two_ref, result_ref, gf_ref, result_out, gf_out, gq_out, go_out, gc_out, gg_out):
-    parts, rows, first = one_ref.shape
-    whole = parts * rows
-    wide = gq_out.shape[1]
+        big[k * step : (k + 1) * step, :, part:] = piece
+    if used < parts:
+        big[used:, :, part:] = jnp.zeros((parts - used, rows, LANES), bf16)
+
+
+def finish(one_ref, three_ref, two_ref, result_ref, gf_ref, result_out, gf_out, gq_out, go_out, gc_out, gg_out):
+    parts, rows, _ = two_ref.shape
     att, channels = go_out.shape
-    fold = whole // att
+    fold = parts * rows // att
     part = channels // fold
-    rest = wide - first
     f32 = jnp.float32
     result_out[...] = result_ref[...]
     gf_out[...] = gf_ref[...]
-    gq_out[:, :first] = one_ref[...].astype(f32).reshape(whole, first)
-    gq_out[:, first:] = two_ref[:, :, :rest].astype(f32).reshape(whole, rest)
+    half = one_ref.shape[2]
+    gq_out[:, :half] = one_ref[...].astype(f32).reshape(parts * rows, half)
+    gq_out[:, half:] = three_ref[...].astype(f32).reshape(parts * rows, half)
     for k in range(fold):
-        piece = two_ref[k * (parts // fold) : (k + 1) * (parts // fold), :, rest : rest + part]
+        piece = two_ref[k * (parts // fold) : (k + 1) * (parts // fold), :, :part]
         go_out[:, k * part : (k + 1) * part] = piece.astype(f32).reshape(att, part)
     step = 64 // rows
     for k in range(channels // LANES):
         lanes = slice(k * LANES, (k + 1) * LANES)
-        small = two_ref[k * step : (k + 1) * step, :, rest + part :].astype(f32).reshape(64, LANES)
+        small = two_ref[k * step : (k + 1) * step, :, part:].astype(f32).reshape(64, LANES)
         for a in range(7):
             gc_out[a, :, lanes] = small[a * 7 : (a + 1) * 7]
         gg_out[:, lanes] = small[49:50]
 
 
-def halving(turns, big, every, got, held, send, recv):
-    f32 = jnp.float32
-    count = len(turns)
-    sizes = [big.shape[0] >> (k + 1) for k in range(count)]
-    base = [0]
-    for n in sizes[:-1]:
-        base.append(base[-1] + n)
-    starts = [jnp.int32(0)]
-    for (_, bit), n in zip(turns, sizes):
-        starts.append(starts[-1] + bit * n)
-
-    def source(k, at, n):
-        return big.at[pl.ds(at, n)] if k == 0 else held.at[pl.ds(base[k - 1] + at, n)]
-
-    def down(k):
-        target, bit = turns[k]
-        n = sizes[k]
-        return remote(
-            source(k, (1 - bit) * n, n), got.at[base[k] : base[k] + n], send.at[k], recv.at[k], target
-        )
-
-    def back(k, mine):
-        target, bit = turns[k]
-        n = sizes[k]
-        spot = every.at[pl.ds(starts[k] + (bit if mine else 1 - bit) * n, n)]
-        return remote(spot, spot, send.at[count + k], recv.at[count + k], target)
-
-    def add(k):
-        bit, n = turns[k][1], sizes[k]
-        down(k).wait()
-        for i in range(n):
-            at = bit * n + i
-            mine = big[at] if k == 0 else held[base[k - 1] + at]
-            total = (mine.astype(f32) + got[base[k] + i].astype(f32)).astype(big.dtype)
-            if k == count - 1:
-                every[starts[count] + i] = total
-            else:
-                held[base[k] + i] = total
-        if k == count - 1:
-            back(k, True).start()
-        else:
-            down(k + 1).start()
-
-    def gather(k):
-        back(k, True).wait_send()
-        back(k, False).wait_recv()
-        if k:
-            back(k - 1, True).start()
-
-    stages = [lambda: down(0).start()]
-    stages += [functools.partial(add, k) for k in range(count)]
-    stages += [functools.partial(gather, k) for k in reversed(range(count))]
-    return stages
-
-
 def give_rows(n_lon, lon, src, dst, send, recv):
     own = src.shape[0]
 
@@ -638,11 +600,89 @@
     return start, wait
 
 
+def sum_stages(sizes, big, all_ref, got1, sum1, got2, sum2, got3, send, recv):
+    n_lat, n_lon, n_dp = sizes
+    lat, lon, dp = place()
+    half, quarter = n_lat * n_lon, n_lon
+    f32 = jnp.float32
+    other_dp, other_lat = 1 - dp, 1 - lat
+    mine = dp * half + lat * quarter
+    one = remote(big.at[pl.ds(other_dp * half, half)], got1, send.at[0], recv.at[0], {"dp": other_dp})
+    two = remote(sum1.at[pl.ds(other_lat * quarter, quarter)], got2, send.at[1], recv.at[1], {"lat": other_lat})
+
+    def three(i, j):
+        return remote(sum2.at[j], got3.at[i], send.at[2 + j], recv.at[2 + i], {"lon": j})
+
+    base = 2 + n_lon
+
+    def four(i, j):
+        spot = all_ref.at[mine + i]
+        return remote(spot, spot, send.at[base + j], recv.at[base + i], {"lon": j})
+
+    base2 = base + n_lon
+
+    def five(side):
+        spot = all_ref.at[pl.ds(dp * half + side * quarter, quarter)]
+        return remote(spot, spot, send.at[base2], recv.at[base2], {"lat": other_lat})
+
+    def six(side):
+        spot = all_ref.at[pl.ds(side * half, half)]
+        return remote(spot, spot, send.at[base2 + 1], recv.at[base2 + 1], {"dp": other_dp})
+
+    def others(do):
+        for j in range(n_lon):
+
+            @pl.when(lon != j)
+            def _(j=j):
+                do(j)
+
+    def s0():
+        one.start()
+
+    def s1():
+        one.wait()
+        for k in range(half):
+            sum1[k] = (big[dp * half + k].astype(f32) + got1[k].astype(f32)).astype(sum1.dtype)
+        two.start()
+
+    def s2():
+        two.wait()
+        for k in range(quarter):
+            sum2[k] = (sum1[lat * quarter + k].astype(f32) + got2[k].astype(f32)).astype(sum2.dtype)
+        others(lambda j: three(lon, j).start())
+        got3[lon] = sum2[lon]
+
+    def s3():
+        others(lambda j: three(j, j).wait_recv())
+        others(lambda j: three(lon, j).wait_send())
+        total = got3[0].astype(f32)
+        for i in range(1, n_lon):
+            total = total + got3[i].astype(f32)
+        all_ref[mine + lon] = total.astype(all_ref.dtype)
+        others(lambda j: four(lon, j).start())
+
+    def s4():
+        others(lambda j: four(j, j).wait_recv())
+        others(lambda j: four(lon, j).wait_send())
+        five(lat).start()
+
+    def s5():
+        five(lat).wait_send()
+        five(other_lat).wait_recv()
+        six(dp).start()
+
+    def s6():
+        six(dp).wait_send()
+        six(other_dp).wait_recv()
+
+    return s0, s1, s2, s3, s4, s5, s6
+
+
 def layer(sizes, f_ref, c_ref, w_hbm, gain_ref, wq_hbm, wo_hbm,
-          result_out, gf_out, every1, every2,
-          fp, cr, weight, wq, wo, pad, update, result, gu, gub, gq, go, gg, top, low, gpad, out, gf, conv,
-          big1, got1, held1, big2, got2, held2,
-          send, recv, xsend, xrecv, local, hsend, hrecv, rsend, rrecv, gsend, grecv, s1, r1, s2, r2):
+          result_out, gf_out, every1, every3, every2,
+          fp, cr, weight, wq, wo, pad, update, result, gu, gub, go, gg, top, low, gpad, out, gf, conv,
+          big1, a1, b1, c1, d1, e1, big3, a3, b3, c3, d3, e3, big2, a2, b2, c2, d2, e2,
+          send, recv, xsend, xrecv, local, hsend, hrecv, rsend, rrecv, gsend, grecv, s1, r1, s3, r3, s2, r2):
     n_lat, n_lon, _ = sizes
     lat, lon, dp = place()
     own, circle, channels = gu.shape
@@ -653,13 +693,9 @@
     ]
     for load in loads:
         load.start()
-    odd, high = lax.rem(lon, 2), lon // 2
-    by_dp = ({"dp": 1 - dp}, dp)
-    by_lat = ({"lat": 1 - lat}, lat)
-    by_odd = ({"lon": lon + 1 - 2 * odd}, odd)
-    by_high = ({"lon": lon + 2 - 4 * high}, high)
-    one = halving((by_dp, by_lat, by_odd, by_high), big1, every1, got1, held1, s1, r1)
-    two = halving((by_dp, by_odd, by_high, by_lat), big2, every2, got2, held2, s2, r2)
+    one = sum_stages(sizes, big1, every1, a1, b1, c1, d1, e1, s1, r1)
+    three = sum_stages(sizes, big3, every3, a3, b3, c3, d3, e3, s3, r3)
+    two = sum_stages(sizes, big2, every2, a2, b2, c2, d2, e2, s2, r2)
     start_in, wait_fields, wait_cot, wait_sent = bring_rows(
         sizes, f_ref, c_ref, fp, cr, send, recv, xsend, xrecv, local
     )
@@ -674,30 +710,33 @@
     convolve(pad, weight, update, own, False)
     for load in loads[1:]:
         load.wait()
-    steps = core_step(cr, update, gain_ref[...], wq, wo, result, gu, gub, gq, go, gg)
+    steps = core_step(cr, update, gain_ref[...], wq, wo, result, gu, gub, big1, big3, go, gg)
     next(steps)
+    start_r()
     wait_cot()
     next(steps)
     start_h()
     next(steps)
-    start_r()
+    one[0]()
+    three[0]()
     next(steps)
     correlate_rows(pad, gu, conv, own)
-    pack((big1, big2), gq, go, conv, gg)
-    one[0]()
+    pack(big2, go, conv, gg)
     two[0]()
+    one[1]()
+    three[1]()
     wait_h()
     gpad[0:3] = top[...].astype(f32).reshape((3, circle, channels))
     gpad[3 : own + 3] = gu[...]
     gpad[own + 3 :] = low[...].astype(f32).reshape((3, circle, channels))
-    one[1]()
-    two[1]()
     convolve(gpad, weight, out, own, True)
     gf[...] = out[...].reshape(gf.shape).astype(bf16)
-    start_g()
-    for stage_one, stage_two in zip(one[2:], two[2:]):
-        stage_one()
-        stage_two()
+    two[1]()
+    for k in range(2, len(one)):
+        for stream in (one, three, two):
+            stream[k]()
+        if k == 3:
+            start_g()
     wait_sent()
     wait_r()
     wait_g()
@@ -714,39 +753,37 @@
     vmem = pltpu.VMEM
     parts = n_lat * n_lon * n_dp
     part_rows = channels // parts
-    wide = w_qkv.shape[1] + att * att // channels * (channels // att) + LANES
-    first = (wide // LANES + 1) // 2 * LANES
-    widths = (first, wide - first)
-    turns = 2 + 2
+    widths = (w_qkv.shape[1] // 2, w_qkv.shape[1] // 2, att + LANES)
+    turns = 4 + 2 * n_lon
     blocked = (own, n_lon, cols, channels)
     flat = (own, circle, channels)
     padded = (own + 6, circle, channels)
     sums = []
     for w in widths:
-        sums += [vmem((n, part_rows, w), bf16) for n in (parts, parts, parts)]
+        sums += [vmem((n, part_rows, w), bf16) for n in (parts, parts // 2, parts // 2, n_lon, n_lon, n_lon)]
     inside = pl.BlockSpec(memory_space=pltpu.VMEM)
     outside = pl.BlockSpec(memory_space=pl.ANY)
-    result, grad_fields, one, two = pl.pallas_call(
+    result, grad_fields, one, three, two = pl.pallas_call(
         functools.partial(layer, sizes),
         out_shape=[shape((rows, cols, channels), bf16)] * 2
         + [shape((parts, part_rows, w), bf16) for w in widths],
         in_specs=[outside, outside, outside, inside, outside, outside],
-        out_specs=[inside] * 4,
+        out_specs=[inside] * 5,
         scratch_shapes=[
             vmem((own + 6,) + blocked[1:], bf16), vmem(blocked, bf16), vmem(conv_weight.shape, f32),
             vmem(w_qkv.shape, bf16), vmem(w_out.shape, bf16),
             vmem(padded, f32), vmem(flat, f32), vmem(blocked, bf16), vmem(flat, f32), vmem(blocked, bf16),
-            vmem(w_qkv.shape, f32), vmem(w_out.shape, f32), vmem((1, channels), f32),
+            vmem(w_out.shape, f32), vmem((1, channels), f32),
             vmem((3,) + blocked[1:], bf16), vmem((3,) + blocked[1:], bf16),
             vmem(padded, f32), vmem(flat, f32), vmem(blocked, bf16), vmem(conv_weight.shape, f32),
         ] + sums + [
             sems((2, n_lon)), sems((2, n_lon)), sems((2,)), sems((2, n_lon)), sems((5,)),
             sems((2,)), sems((2,)),
             sems((n_lon,)), sems((n_lon,)), sems((n_lon,)), sems((n_lon,)),
-            sems((2 * turns,)), sems((2 * turns,)), sems((2 * turns,)), sems((2 * turns,)),
+            sems((turns,)), sems((turns,)), sems((turns,)), sems((turns,)), sems((turns,)), sems((turns,)),
         ],
         compiler_params=pltpu.CompilerParams(
-            vmem_limit_bytes=48 * 2**20, collective_id=1, has_side_effects=True
+            vmem_limit_bytes=67043328, collective_id=1, has_side_effects=True
         ),
     )(fields[0], cotangent[0], conv_weight, norm_gain.reshape(1, channels), w_qkv, w_out)
     outs = pl.pallas_call(
@@ -754,10 +791,10 @@
         out_shape=[shape((rows, cols, channels), bf16)] * 2
         + [shape(w_qkv.shape, f32), shape(w_out.shape, f32), shape(conv_weight.shape, f32),
            shape((1, channels), f32)],
-        in_specs=[inside] * 4,
+        in_specs=[inside] * 5,
         out_specs=[inside] * 6,
-        compiler_params=pltpu.CompilerParams(vmem_limit_bytes=32 * 2**20),
-    )(one, two, result, grad_fields)
+        compiler_params=pltpu.CompilerParams(vmem_limit_bytes=67043328),
+    )(one, three, two, result, grad_fields)
     return outs[0][None], outs[1][None], outs[2], outs[3], outs[4], outs[5].reshape(channels)
 
 
@@ -772,7 +809,7 @@
         and rows % n_lon == 0 and rows // n_lon >= 3 and cols % 8 == 0
         and LANES % (cols * n_lon) == 0 and (rows // n_lon * cols * n_lon) % LANES == 0
         and channels == 2 * att and channels % (8 * parts) == 0 and 64 % (channels // parts) == 0
-        and att % LANES == 0
+        and att % LANES == 0 and args[4].shape[1] == 3 * att and 3 * att % (2 * LANES) == 0
     )
     return on_device(sizes, *args) if fits else on_device_native(*args)
 

time: 73.5 us -> 65.6 us (0.89)
  local copies, waits for them, and re-layouts: 5.55 us -> 0 us
  Pallas kernels: 67 us -> 64.8 us
    unnamed x12 -> x0, local copies, waits for them, and re-layouts: 5.55 us -> none
    pallas_call x1, Pallas kernels: 65.4 us -> 61.9 us  [on_device(): pl.pallas_call(functools.partial(layer, sizes), out_shape=[shape((rows, c...]
    pallas_call x1, Pallas kernels: 1.65 us -> 2.92 us  [on_device(): pl.pallas_call(finish, out_shape=[shape((rows, cols, channels), bf16)] *...]
where the time goes in v3:
time: 65.6 us; the launch traced here: 65.4 us
  Pallas kernels  64.8 us (99%)
    pallas_call x1, Pallas kernels, on_device(): pl.pallas_call(functools.partial(layer, sizes), out_shape=[shape((rows, c...  61.9 us
    pallas_call x1, Pallas kernels, on_device(): pl.pallas_call(finish, out_shape=[shape((rows, cols, channels), bf16)] *...  2.92 us

profile of v3, /device:TPU:0, one launch (start us, length us, event | category | flops | bytes accessed | tf_op | source)
XLA Modules:
  0.0 65.4 jit_solution(3850749806460512398)
XLA Ops:
  0.6 61.9 %shard_map.109 = (bf16[32,8,512]{2,1,0:T(8,128)(2,1)}, bf16[32,8,512]{2,1,0:T(8,128)(2,1)}, bf16[16,32,384]{2,1,0:T(8,128)(2,1)}, bf16[16,32,384]{2,1,0:T(8,128)(2,1)}, bf16[16,32,384]{2,1,0:T(8,128)(2,1)}) custom-call(bf16[32,8,512]{2,1,0:T(8,128)(2,1)} %bitcast.6, bf16[32,8,512]{2,1,0:T(8,128)(2,1)} %bitcast.7, f32[7,7,512]{2,1,0:T(8,128)} %w_hbm.1, ...), custom_call_target="tpu_custom_call" | custom-call | tf_op jit(solution)/shard_map/pallas_call | solution.py:766
  62.5 2.9 %shard_map.110 = (bf16[32,8,512]{2,1,0:T(8,128)(2,1)}, bf16[32,8,512]{2,1,0:T(8,128)(2,1)}, f32[512,768]{1,0:T(8,128)}, f32[256,512]{1,0:T(8,128)}, f32[7,7,512]{2,1,0:T(8,128)}, /*index=5*/f32[1,512]{1,0:T(1,128)}) custom-call(bf16[16,32,384]{2,1,0:T(8,128)(2,1)} %get-tuple-element.17.one_ref, bf16[16,32,384]{2,1,0:T(8,128)(2,1)} %get-tuple-element.18.three_ref, ...), custom_call_target="tpu_custom_call" | custom-call | tf_op jit(solution)/shard_map/pallas_call | solution.py:789
